TPU v7x, 32 devices: a whole 2x2x4 slice. The times are simulated.
32 devices in a mesh: trow: 8 (over y, x, core), tcol: 4 (over z).
Axes of the slice: x: 2, y: 2, z: 4, core: 2. Of those that a mesh axis runs over, the one named last changes fastest.
Arguments:
- theta: float32 [25, 128, 1024], P(None, 'trow', 'tcol'), may hold values from -6 to 6
- salt: float32 [25, 128, 1024], P(None, 'trow', 'tcol'), may hold values from -6 to 6
- velocity_x: float32 [25, 128, 1024], P(None, 'trow', 'tcol'), may hold values from -0.5 to 0.5
- velocity_y: float32 [25, 128, 1024], P(None, 'trow', 'tcol'), may hold values from -0.5 to 0.5
- land_mask: int32 [25, 128, 1024], P(None, 'trow', 'tcol'), may hold values 0 or 1
- kappa: float32 [24, 128, 1024], P(None, 'trow', 'tcol'), may hold values from 0.02 to 5
- forcing: float32 [128, 1024], P('trow', 'tcol'), may hold values from -6 to 6
- bottom: int32 [128, 1024], P('trow', 'tcol'), may hold values from 0 to 25
- theta_cot: float32 [25, 128, 1024], P(None, 'trow', 'tcol'), may hold values from -6 to 6
- salt_cot: float32 [25, 128, 1024], P(None, 'trow', 'tcol'), may hold values from -6 to 6
- surface_cot: float32 [128, 1024], P('trow', 'tcol'), may hold values from -24 to 24
Outputs:
- theta_grad: float32 [25, 128, 1024], P(None, 'trow', 'tcol')
- salt_grad: float32 [25, 128, 1024], P(None, 'trow', 'tcol')
- kappa_grad: float32 [24, 128, 1024], P(None, 'trow', 'tcol')
- forcing_grad: float32 [128, 1024], P('trow', 'tcol')
All inputs are finite; a program needn't handle non-finite values. No bound on the sum of `land_mask` on one device may be relied on, other than what follows from the above.
Results may differ from a plain program's by a relative error of at most 0.0001.
Values sent between devices are 32-bit elements; how exact they have to be, the bound alone decides.
A program may use at most 64 MiB of HBM per device.

v0:
```python
import jax
import jax.numpy as jnp
from jax import lax
from jax.sharding import PartitionSpec as P

ITERS = 4


def padded_2(array, sides, width):
    for axis, dim in sides:
        peers, length = (lax.axis_size(axis), array.shape[dim])
        up = [(i, (i + 1) % peers) for i in range(peers - 1)]
        down = [(j, i) for i, j in up]
        last = lax.slice_in_dim(array, length - width, length, axis=dim)
        leading = lax.slice_in_dim(array, 0, width, axis=dim)
        before = lax.ppermute(last, axis, up)
        after = lax.ppermute(leading, axis, down)
        array = jnp.concatenate([before, array, after], axis=dim)
    return array


def cut_along(array, start, count, axis_index):
    return lax.slice_in_dim(array, start, start + count, axis=axis_index)


def forward_change(padded_tracer, padded_velocity, padded_wet, axis_index, length):
    opened = (
        cut_along(padded_velocity, 1, length + 1, axis_index)
        * cut_along(padded_wet, 1, length + 1, axis_index)
        * cut_along(padded_wet, 2, length + 1, axis_index)
    )
    centre = cut_along(padded_tracer, 1, length + 1, axis_index) + cut_along(
        padded_tracer, 2, length + 1, axis_index
    )
    outer = cut_along(padded_tracer, 0, length + 1, axis_index) + cut_along(
        padded_tracer, 3, length + 1, axis_index
    )
    fluxes = opened * (7.0 * centre - outer) / 12.0
    return cut_along(fluxes, 1, length, axis_index) - cut_along(fluxes, 0, length, axis_index)


def adjoint_change(padded_lambda, padded_velocity, padded_wet, axis_index, length):
    opened = (
        cut_along(padded_velocity, 0, length + 3, axis_index)
        * cut_along(padded_wet, 0, length + 3, axis_index)
        * cut_along(padded_wet, 1, length + 3, axis_index)
    )
    faces = opened * (
        cut_along(padded_lambda, 0, length + 3, axis_index)
        - cut_along(padded_lambda, 1, length + 3, axis_index)
    )
    return (
        7.0 * (cut_along(faces, 2, length, axis_index) + cut_along(faces, 1, length, axis_index))
        - cut_along(faces, 3, length, axis_index)
        - cut_along(faces, 0, length, axis_index)
    ) / 12.0


def advect(padded_tracer, padded_ux, padded_uy, padded_wet, tracer):
    row_count = padded_tracer.shape[1] - 4
    col_count = padded_tracer.shape[2] - 4
    along_rows = forward_change(
        padded_tracer[:, :, 2:-2], padded_ux[:, :, 2:-2], padded_wet[:, :, 2:-2], 1, row_count
    )
    along_cols = forward_change(
        padded_tracer[:, 2:-2, :], padded_uy[:, 2:-2, :], padded_wet[:, 2:-2, :], 2, col_count
    )
    return tracer - along_rows - along_cols


def advect_adjoint(padded_lambda, padded_ux, padded_uy, padded_wet, lambda_field, wet):
    row_count = padded_lambda.shape[1] - 4
    col_count = padded_lambda.shape[2] - 4
    along_rows = adjoint_change(
        padded_lambda[:, :, 2:-2], padded_ux[:, :, 2:-2], padded_wet[:, :, 2:-2], 1, row_count
    )
    along_cols = adjoint_change(
        padded_lambda[:, 2:-2, :], padded_uy[:, 2:-2, :], padded_wet[:, 2:-2, :], 2, col_count
    )
    return lambda_field - wet * (along_rows + along_cols)


def factorize(couple, depth):
    inverses = []
    ratios = []
    for depth_index in range(depth):
        diagonal = jnp.ones_like(couple[0])
        if depth_index > 0:
            diagonal = (
                diagonal
                + couple[depth_index - 1]
                - couple[depth_index - 1] * ratios[depth_index - 1]
            )
        if depth_index < depth - 1:
            diagonal = diagonal + couple[depth_index]
        inverse = 1.0 / diagonal
        inverses.append(inverse)
        if depth_index < depth - 1:
            ratios.append(couple[depth_index] * inverse)
    return (inverses, ratios)


def solve_columns(inverses, ratios, couple, rhs):
    depth = rhs.shape[0]
    sweeps = []
    carried = rhs[0] * inverses[0]
    sweeps.append(carried)
    for depth_index in range(1, depth):
        carried = (rhs[depth_index] + couple[depth_index - 1] * carried) * inverses[depth_index]
        sweeps.append(carried)
    results = [sweeps[depth - 1]]
    for depth_index in range(depth - 2, -1, -1):
        results.append(sweeps[depth_index] + ratios[depth_index] * results[-1])
    return jnp.stack(results[::-1])


LOW, HIGH = 0.2, 9.2
CENTRE, RADIUS = (HIGH + LOW) / 2, (HIGH - LOW) / 2


def times_operator(poly):
    out = [0.0] * (len(poly) + 1)
    for k, c in enumerate(poly):
        out[k] = out[k] + CENTRE * c
        if k == 0:
            out[1] = out[1] + RADIUS * c
        else:
            out[k + 1] = out[k + 1] + 0.5 * RADIUS * c
            out[k - 1] = out[k - 1] + 0.5 * RADIUS * c
    return out


def inner(p, q, moments):
    total = 0.0
    for i, a in enumerate(p):
        for j, b in enumerate(q):
            total = total + a * b * (0.5 * (moments[i + j] + moments[abs(i - j)]))
    return total


def add_scaled(p, scale, q):
    size = max(len(p), len(q))
    p = p + [0.0] * (size - len(p))
    q = q + [0.0] * (size - len(q))
    return [a + scale * b for a, b in zip(p, q)]


def weights_from(moments):
    residual = [jnp.ones_like(moments[0])]
    direction = residual
    result = []
    norm_now = moments[0]
    for iteration in range(ITERS):
        image = times_operator(direction)
        step = norm_now / inner(direction, image, moments)
        result = add_scaled(result, step, direction)
        if iteration + 1 < ITERS:
            residual = add_scaled(residual, -step, image)
            norm_next = inner(residual, residual, moments)
            direction = add_scaled(residual, norm_next / norm_now, direction)
            norm_now = norm_next
    return result


def conjugate(target, bottom, depth):
    rows, cols = target.shape
    rim = ITERS
    padded = padded_2(jnp.stack([target, bottom.astype(jnp.float32)]), (("trow", 1), ("tcol", 2)), rim)
    row = lax.broadcasted_iota(jnp.int32, (rows + 2 * rim, 1), 0) - rim + lax.axis_index("trow") * rows
    col = lax.broadcasted_iota(jnp.int32, (1, cols + 2 * rim), 1) - rim + lax.axis_index("tcol") * cols
    inside = ((row >= 0) & (row < rows * lax.axis_size("trow"))) & (
        (col >= 0) & (col < cols * lax.axis_size("tcol"))
    )
    scaled = (4.2 - CENTRE + padded[1] / depth) / RADIUS
    basis = [padded[0]]
    for k in range(ITERS):
        field = basis[-1]
        edge = k + 1
        beside = field[2:, 1:-1] + field[:-2, 1:-1] + field[1:-1, 2:] + field[1:-1, :-2]
        image = scaled[edge:-edge, edge:-edge] * field[1:-1, 1:-1] - beside * (1.0 / RADIUS)
        if k > 0:
            image = 2.0 * image - basis[-2][2:-2, 2:-2]
        basis.append(jnp.where(inside[edge:-edge, edge:-edge], image, 0.0))
    own = [f[rim - k : rim - k + rows, rim - k : rim - k + cols] for k, f in enumerate(basis)]
    sums = [jnp.sum(own[0] * own[k]) for k in range(5)]
    sums += [jnp.sum(own[2] * own[3]), jnp.sum(own[3] * own[3]), jnp.sum(own[3] * own[4])]
    m = list(lax.psum(jnp.stack(sums), ("trow", "tcol")))
    m = m[:5] + [2.0 * m[5] - m[1], 2.0 * m[6] - m[0], 2.0 * m[7] - m[1]]
    weights = weights_from(m)
    result = weights[0] * own[0]
    for k in range(1, ITERS):
        result = result + weights[k] * own[k]
    return result


def forward_state(padded, theta, salt, forcing, wet, inverses, ratios, couple):
    theta_adv = advect(padded[0], padded[2], padded[3], padded[4], theta)
    salt_adv = advect(padded[1], padded[2], padded[3], padded[4], salt)
    source = jnp.concatenate([theta_adv[:1] + (forcing * wet[0])[None], theta_adv[1:]], axis=0)
    theta_mix = solve_columns(inverses, ratios, couple, source)
    salt_mix = solve_columns(inverses, ratios, couple, salt_adv)
    return (theta_mix, salt_mix)


def mixing_adjoint(zeta, wet, theta_cot, salt_cot, inverses, ratios, couple):
    theta_total = theta_cot + 0.2 * wet * zeta[None]
    salt_total = salt_cot - 0.15 * wet * zeta[None]
    theta_mu = solve_columns(inverses, ratios, couple, theta_total)
    salt_mu = solve_columns(inverses, ratios, couple, salt_total)
    return (theta_mu, salt_mu)


def shards(
    theta,
    salt,
    velocity_x,
    velocity_y,
    land_mask,
    kappa,
    forcing,
    bottom,
    theta_cot,
    salt_cot,
    surface_cot,
):
    depth = theta.shape[0]
    levels = lax.broadcasted_iota(jnp.int32, (depth, 1, 1), 0)
    wet = land_mask.astype(jnp.float32) * (levels < bottom[None]).astype(jnp.float32)
    couple = [
        kappa[depth_index] * wet[depth_index] * wet[depth_index + 1]
        for depth_index in range(depth - 1)
    ]
    inverses, ratios = factorize(couple, depth)
    stacked = jnp.stack([theta * wet, salt * wet, velocity_x, velocity_y, wet])
    padded = padded_2(stacked, (("trow", 2), ("tcol", 3)), 2)
    theta_mix, salt_mix = forward_state(padded, theta, salt, forcing, wet, inverses, ratios, couple)
    zeta = conjugate(surface_cot, bottom, depth)
    theta_mu, salt_mu = mixing_adjoint(zeta, wet, theta_cot, salt_cot, inverses, ratios, couple)
    lambdas = padded_2(jnp.stack([theta_mu, salt_mu]), (("trow", 2), ("tcol", 3)), 2)
    padded_theta_mu = lambdas[0]
    padded_salt_mu = lambdas[1]
    opened = wet[:-1] * wet[1:]
    kappa_grad = -opened * (
        (theta_mu[:-1] - theta_mu[1:]) * (theta_mix[:-1] - theta_mix[1:])
        + (salt_mu[:-1] - salt_mu[1:]) * (salt_mix[:-1] - salt_mix[1:])
    )
    forcing_grad = zeta + wet[0] * theta_mu[0]
    theta_grad = advect_adjoint(padded_theta_mu, padded[2], padded[3], padded[4], theta_mu, wet)
    salt_grad = advect_adjoint(padded_salt_mu, padded[2], padded[3], padded[4], salt_mu, wet)
    return (theta_grad, salt_grad, kappa_grad, forcing_grad)


def solution(mesh):
    in_specs = (
        P(None, "trow", "tcol"),
        P(None, "trow", "tcol"),
        P(None, "trow", "tcol"),
        P(None, "trow", "tcol"),
        P(None, "trow", "tcol"),
        P(None, "trow", "tcol"),
        P("trow", "tcol"),
        P("trow", "tcol"),
        P(None, "trow", "tcol"),
        P(None, "trow", "tcol"),
        P("trow", "tcol"),
    )
    out_specs = (
        P(None, "trow", "tcol"),
        P(None, "trow", "tcol"),
        P(None, "trow", "tcol"),
        P("trow", "tcol"),
    )
    return jax.shard_map(shards, mesh=mesh, in_specs=in_specs, out_specs=out_specs, check_vma=False)
```

profile of v0, /device:TPU:3, one launch (start us, length us, event | category | flops | bytes accessed | tf_op | source)
XLA Modules:
  0.0 165.0 jit_solution(13457060949592738381)
XLA Ops:
  4.1 3.7 %collective-permute-start.4 = (f32[5,25,2,256]{3,2,1,0:T(2,128)}, f32[5,25,2,256]{3,2,1,0:T(2,128)S(1)}, u32[]{:S(2)}, u32[]{:S(2)}) collective-permute-start(f32[5,25,2,256]{3,2,1,0:T(2,128)} %get-tuple-element.286), channel_id=1, source_target_pairs={{0,4},{4,8},{8,12},{12,16},{16,20},{20,24},{24,28},{1,5},{5,9},{9,... | collective-permute-start | bytes 768008 | tf_op jit(solution)/shard_map/ppermute | solution.py:16
  7.8 1.9 %collective-permute-start = (f32[2,4,256]{2,1,0:T(4,128)S(1)}, f32[2,4,256]{2,1,0:T(4,128)S(1)}, u32[]{:S(2)}, u32[]{:S(2)}) collective-permute-start(f32[2,4,256]{2,1,0:T(4,128)S(1)} %get-tuple-element.320), channel_id=1, source_target_pairs={{0,4},{4,8},{8,12},{12,16},{16,20},{20,24},{24,28},{1,5},{5,9},{9,... | collective-permute-start | bytes 24584 | tf_op jit(solution)/shard_map/ppermute | solution.py:16
  9.8 2.4 %collective-permute-start.1 = (f32[2,4,256]{2,1,0:T(4,128)S(1)}, f32[2,4,256]{2,1,0:T(4,128)S(1)}, u32[]{:S(2)}, u32[]{:S(2)}) collective-permute-start(f32[2,4,256]{2,1,0:T(4,128)S(1)} %get-tuple-element.321), channel_id=1, source_target_pairs={{4,0},{8,4},{12,8},{16,12},{20,16},{24,20},{28,24},{5,1},{9,5},{13... | collective-permute-start | bytes 24584 | tf_op jit(solution)/shard_map/ppermute | solution.py:17
  12.2 3.4 %collective-permute-done.1 = f32[2,4,256]{2,1,0:T(4,128)S(1)} collective-permute-done((f32[2,4,256]{2,1,0:T(4,128)S(1)}, f32[2,4,256]{2,1,0:T(4,128)S(1)}, u32[]{:S(2)}, u32[]{:S(2)}) %collective-permute-start.1) | collective-permute-done | bytes 8224 | tf_op jit(solution)/shard_map/ppermute | solution.py:17
  15.7 3.2 %collective-permute-start.2 = (f32[2,24,4]{2,1,0:T(8,128)S(1)}, f32[2,24,4]{2,1,0:T(8,128)S(1)}, u32[]{:S(2)}, u32[]{:S(2)}) collective-permute-start(f32[2,24,4]{2,1,0:T(8,128)S(1)} %get-tuple-element.318), channel_id=1, source_target_pairs={{0,1},{1,2},{2,3},{4,5},{5,6},{6,7},{8,9},{9,10},{10,11},{12,13},{... | collective-permute-start | bytes 2312 | tf_op jit(solution)/shard_map/ppermute | solution.py:16
  20.3 3.2 %collective-permute-done.3 = f32[2,24,4]{2,1,0:T(8,128)S(1)} collective-permute-done((f32[2,24,4]{2,1,0:T(8,128)S(1)}, f32[2,24,4]{2,1,0:T(8,128)S(1)}, u32[]{:S(2)}, u32[]{:S(2)}) %collective-permute-start.3) | collective-permute-done | bytes 800 | tf_op jit(solution)/shard_map/ppermute | solution.py:17
  24.9 5.1 %stack.73 = f32[8]{0:T(128)S(1)} concatenate(f32[1]{0:T(128)} %bitcast.3, f32[1]{0:T(128)} %bitcast.5, f32[1]{0:T(128)} %bitcast.6, f32[1]{0:T(128)} %bitcast.7, f32[1]{0:T(128)} %bitcast.8, f32[1]{0:T(128)} %bitcast.9, f32[1]{0:T(128)} %bitcast.10, f32[1]{0:T(128)} %bitcast.11), dimensions={0} | concatenate | bytes 64 | tf_op jit(solution)/shard_map/stack | solution.py:187
  31.8 40.4 %psum.7 = f32[8]{0:T(128)S(1)} all-reduce(f32[8]{0:T(128)S(1)} %stack.73), channel_id=1, replica_groups=mesh['trow'=8,'tcol'=4] {'trow','tcol'}, use_global_device_ids=true, to_apply=%region_8.9 | all-reduce | flops 8 | bytes 64 | tf_op jit(solution)/shard_map/psum | solution.py:187
  92.9 2.0 %multiply_add_fusion = (f32[25,16,256]{2,1,0:T(8,128)S(1)}, f32[25,16,256]{2,1,0:T(8,128)}) fusion(f32[25,16,256]{2,1,0:T(8,128)} %param.19, f32[25,16,256]{2,1,0:T(8,128)S(1)} %get-tuple-element.227, f32[16,256]{1,0:T(8,128)S(1)} %broadcast_multiply_fusion.1, f32[25,16,256]{2,1,0:T(8,128)} %param.20, f32[16,256]{1,0:T(8,128)S(1)} %get-tuple-element.254), kind=kLoop, calls=%fused_computation.331 | loop fusion | flops 409600 | bytes 2080768 | tf_op jit(solution)/shard_map/add | solution.py:206
  96.5 2.1 %fusion.252 = (f32[5,25,20,2]{3,2,1,0:T(8,128)}, f32[5,25,20,2]{3,2,1,0:T(8,128)}) fusion(f32[5,25,20,256]{3,2,1,0:T(8,128)S(1)} %pad_maximum_fusion.1), kind=kLoop, calls=%fused_computation.842 | loop fusion | bytes 80000 | tf_op jit(solution)/shard_map/slice | solution.py:14
  98.6 2.2 %copy.255 = f32[5,25,20,2]{1,3,2,0:T(2,128)S(1)} copy(f32[5,25,20,2]{3,2,1,0:T(8,128)} %get-tuple-element.284) | data formatting | bytes 40000 | tf_op jit(solution)/shard_map/slice | solution.py:14
  100.8 2.5 %collective-permute-start.6 = (f32[5,25,20,2]{1,3,2,0:T(2,128)S(1)}, f32[5,25,20,2]{1,3,2,0:T(2,128)}, u32[]{:S(2)}, u32[]{:S(2)}) collective-permute-start(f32[5,25,20,2]{1,3,2,0:T(2,128)S(1)} %copy.255), channel_id=1, source_target_pairs={{0,1},{1,2},{2,3},{4,5},{5,6},{6,7},{8,9},{9,10},{10,11},{12,13},{... | collective-permute-start | bytes 60008 | tf_op jit(solution)/shard_map/ppermute | solution.py:16
  103.3 2.7 %copy.256 = f32[5,25,20,2]{1,3,2,0:T(2,128)} copy(f32[5,25,20,2]{3,2,1,0:T(8,128)} %get-tuple-element.285) | data formatting | bytes 40000 | tf_op jit(solution)/shard_map/slice | solution.py:15
  108.4 2.9 %copy.257 = f32[5,25,20,2]{3,2,1,0:T(8,128)} copy(f32[5,25,20,2]{1,3,2,0:T(2,128)} %collective-permute-done.6) | data formatting | bytes 40000 | tf_op jit(solution)/shard_map/ppermute | solution.py:16
  111.7 2.8 %copy.258 = f32[5,25,20,2]{3,2,1,0:T(8,128)} copy(f32[5,25,20,2]{1,3,2,0:T(2,128)} %collective-permute-done.7) | data formatting | bytes 40000 | tf_op jit(solution)/shard_map/ppermute | solution.py:17
  114.5 4.6 %pad_maximum_fusion = f32[5,25,20,260]{3,2,1,0:T(8,128)S(1)} fusion(f32[5,25,20,2]{3,2,1,0:T(8,128)} %copy.258, f32[5,25,2,256]{3,2,1,0:T(2,128)} %collective-permute-done.5, f32[5,25,16,256]{3,2,1,0:T(8,128)S(1)} %constant_dynamic-update-slice_fusion.25, f32[5,25,2,256]{3,2,1,0:T(2,128)S(1)} %copy-done.8, f32[5,25,20,2]{3,2,1,0:T(8,128)} %copy.257), kind=kLoop, calls=%fused_computation | loop fusion | flops 2600000 | bytes 5200000 | tf_op jit(solution)/shard_map/concatenate | solution.py:18
  128.5 7.0 %collective-permute-start.8 = (f32[2,25,2,256]{3,2,1,0:T(2,128)S(1)}, f32[2,25,2,256]{3,2,1,0:T(2,128)S(1)}, u32[]{:S(2)}, u32[]{:S(2)}) collective-permute-start(f32[2,25,2,256]{3,2,1,0:T(2,128)S(1)} %get-tuple-element.300), channel_id=1, source_target_pairs={{0,4},{4,8},{8,12},{12,16},{16,20},{20,24},{24,28},{1,5},{5,9},{9,... | collective-permute-start | bytes 307208 | tf_op jit(solution)/shard_map/ppermute | solution.py:16
  135.5 1.9 %collective-permute-start.9 = (f32[2,25,2,256]{3,2,1,0:T(2,128)S(1)}, f32[2,25,2,256]{3,2,1,0:T(2,128)S(1)}, u32[]{:S(2)}, u32[]{:S(2)}) collective-permute-start(f32[2,25,2,256]{3,2,1,0:T(2,128)S(1)} %get-tuple-element.301), channel_id=1, source_target_pairs={{4,0},{8,4},{12,8},{16,12},{20,16},{24,20},{28,24},{5,1},{9,5},{13... | collective-permute-start | bytes 307208 | tf_op jit(solution)/shard_map/ppermute | solution.py:17
  138.2 4.2 %collective-permute-done.9 = f32[2,25,2,256]{3,2,1,0:T(2,128)S(1)} collective-permute-done((f32[2,25,2,256]{3,2,1,0:T(2,128)S(1)}, f32[2,25,2,256]{3,2,1,0:T(2,128)S(1)}, u32[]{:S(2)}, u32[]{:S(2)}) %collective-permute-start.9) | collective-permute-done | bytes 102432 | tf_op jit(solution)/shard_map/ppermute | solution.py:17
  145.3 2.7 %collective-permute-start.10 = (f32[2,25,20,2]{1,3,2,0:T(2,128)S(1)}, f32[2,25,20,2]{1,3,2,0:T(2,128)S(1)}, u32[]{:S(2)}, u32[]{:S(2)}) collective-permute-start(f32[2,25,20,2]{1,3,2,0:T(2,128)S(1)} %copy.259), channel_id=1, source_target_pairs={{0,1},{1,2},{2,3},{4,5},{5,6},{6,7},{8,9},{9,10},{10,11},{12,13},{... | collective-permute-start | bytes 24008 | tf_op jit(solution)/shard_map/ppermute | solution.py:16
  148.0 2.0 %copy.260 = f32[2,25,20,2]{1,3,2,0:T(2,128)} copy(f32[2,25,20,2]{3,2,1,0:T(8,128)} %get-tuple-element.299) | data formatting | bytes 16000 | tf_op jit(solution)/shard_map/slice | solution.py:15
  151.5 2.9 %fusion.37 = f32[24,16,256]{2,1,0:T(8,128)} fusion(f32[25,16,256]{2,1,0:T(8,128)S(1)} %get-tuple-element.227, f32[24,16,256]{2,1,0:T(8,128)} %copy-done.15, f32[24,16,256]{2,1,0:T(8,128)} %copy-done.12, f32[24,16,256]{2,1,0:T(8,128)} %copy-done.17, f32[24,16,256]{2,1,0:T(8,128)} %copy-done.11, f32[24,16,256]{2,1,0:T(8,128)} %copy-done.16, ...), kind=kLoop, calls=%fused_computation.336 | loop fusion | flops 983040 | bytes 4325376 | tf_op jit(solution)/shard_map/mul | solution.py:243
  155.6 2.0 %copy.262 = f32[2,25,20,2]{3,2,1,0:T(8,128)} copy(f32[2,25,20,2]{1,3,2,0:T(2,128)} %collective-permute-done.11) | data formatting | bytes 16000 | tf_op jit(solution)/shard_map/ppermute | solution.py:17
  157.6 2.4 %pad_maximum_fusion.2 = f32[2,25,20,260]{3,2,1,0:T(8,128)S(1)} fusion(f32[2,25,20,2]{3,2,1,0:T(8,128)} %copy.262, f32[2,25,2,256]{3,2,1,0:T(2,128)} %copy-done.21, f32[1,25,16,256]{3,2,1,0:T(8,128)S(1)} %bitcast.581, f32[1,25,16,256]{3,2,1,0:T(8,128)S(1)} %bitcast.578, f32[2,25,2,256]{3,2,1,0:T(2,128)} %copy-done.20, f32[2,25,20,2]{3,2,1,0:T(8,128)} %copy.261), kind=kLoop, calls=%fused_computation.2 | loop fusion | flops 1300000 | bytes 2080000 | tf_op jit(solution)/shard_map/concatenate | solution.py:18
  (248 shorter events, 32.6 us)
Async XLA Ops:
  0.6 2.4 %copy-start.18 = (f32[25,16,256]{2,1,0:T(8,128)S(1)}, f32[25,16,256]{2,1,0:T(8,128)}, u32[]{:S(2)}) copy-start(f32[25,16,256]{2,1,0:T(8,128)} %param.13) | copy-start | bytes 1228804
  0.6 2.4 %copy-start.19 = (f32[25,16,256]{2,1,0:T(8,128)S(1)}, f32[25,16,256]{2,1,0:T(8,128)}, u32[]{:S(2)}) copy-start(f32[25,16,256]{2,1,0:T(8,128)} %param.14) | copy-start | bytes 1228804
  3.0 4.8 %copy-start.23 = (s32[16,256]{1,0:T(8,128)S(1)}, s32[16,256]{1,0:T(8,128)}, u32[]{:S(2)}) copy-start(s32[16,256]{1,0:T(8,128)} %param.18) | copy-start | bytes 49156
  3.0 4.8 %copy-start.22 = (f32[16,256]{1,0:T(8,128)S(1)}, f32[16,256]{1,0:T(8,128)}, u32[]{:S(2)}) copy-start(f32[16,256]{1,0:T(8,128)} %param.21) | copy-start | bytes 49156
  4.1 90.8 %collective-permute-start.4 = (f32[5,25,2,256]{3,2,1,0:T(2,128)}, f32[5,25,2,256]{3,2,1,0:T(2,128)S(1)}, u32[]{:S(2)}, u32[]{:S(2)}) collective-permute-start(f32[5,25,2,256]{3,2,1,0:T(2,128)} %get-tuple-element.286), channel_id=1, source_target_pairs={{0,4},{4,8},{8,12},{12,16},{16,20},{20,24},{24,28},{1,5},{5,9},{9,... | collective-permute-start | bytes 768008 | tf_op jit(solution)/shard_map/ppermute | solution.py:16
  7.8 4.4 %collective-permute-start = (f32[2,4,256]{2,1,0:T(4,128)S(1)}, f32[2,4,256]{2,1,0:T(4,128)S(1)}, u32[]{:S(2)}, u32[]{:S(2)}) collective-permute-start(f32[2,4,256]{2,1,0:T(4,128)S(1)} %get-tuple-element.320), channel_id=1, source_target_pairs={{0,4},{4,8},{8,12},{12,16},{16,20},{20,24},{24,28},{1,5},{5,9},{9,... | collective-permute-start | bytes 24584 | tf_op jit(solution)/shard_map/ppermute | solution.py:16
  9.8 5.9 %collective-permute-start.1 = (f32[2,4,256]{2,1,0:T(4,128)S(1)}, f32[2,4,256]{2,1,0:T(4,128)S(1)}, u32[]{:S(2)}, u32[]{:S(2)}) collective-permute-start(f32[2,4,256]{2,1,0:T(4,128)S(1)} %get-tuple-element.321), channel_id=1, source_target_pairs={{4,0},{8,4},{12,8},{16,12},{20,16},{24,20},{28,24},{5,1},{9,5},{13... | collective-permute-start | bytes 24584 | tf_op jit(solution)/shard_map/ppermute | solution.py:17
  15.7 4.6 %collective-permute-start.2 = (f32[2,24,4]{2,1,0:T(8,128)S(1)}, f32[2,24,4]{2,1,0:T(8,128)S(1)}, u32[]{:S(2)}, u32[]{:S(2)}) collective-permute-start(f32[2,24,4]{2,1,0:T(8,128)S(1)} %get-tuple-element.318), channel_id=1, source_target_pairs={{0,1},{1,2},{2,3},{4,5},{5,6},{6,7},{8,9},{9,10},{10,11},{12,13},{... | collective-permute-start | bytes 2312 | tf_op jit(solution)/shard_map/ppermute | solution.py:16
  18.9 4.6 %collective-permute-start.3 = (f32[2,24,4]{2,1,0:T(8,128)S(1)}, f32[2,24,4]{2,1,0:T(8,128)S(1)}, u32[]{:S(2)}, u32[]{:S(2)}) collective-permute-start(f32[2,24,4]{2,1,0:T(8,128)S(1)} %get-tuple-element.319), channel_id=1, source_target_pairs={{1,0},{2,1},{3,2},{5,4},{6,5},{7,6},{9,8},{10,9},{11,10},{13,12},{... | collective-permute-start | bytes 2312 | tf_op jit(solution)/shard_map/ppermute | solution.py:17
  29.9 65.0 %collective-permute-start.5 = (f32[5,25,2,256]{3,2,1,0:T(2,128)}, f32[5,25,2,256]{3,2,1,0:T(2,128)}, u32[]{:S(2)}, u32[]{:S(2)}) collective-permute-start(f32[5,25,2,256]{3,2,1,0:T(2,128)} %get-tuple-element.287), channel_id=1, source_target_pairs={{4,0},{8,4},{12,8},{16,12},{20,16},{24,20},{28,24},{5,1},{9,5},{13... | collective-permute-start | bytes 768008 | tf_op jit(solution)/shard_map/ppermute | solution.py:17
  98.6 8.8 %copy-start.5 = (f32[24,16,256]{2,1,0:T(8,128)S(1)}, f32[24,16,256]{2,1,0:T(8,128)}, u32[]{:S(2)}) copy-start(f32[24,16,256]{2,1,0:T(8,128)} %param.16) | copy-start | bytes 1179652
  100.8 7.6 %collective-permute-start.6 = (f32[5,25,20,2]{1,3,2,0:T(2,128)S(1)}, f32[5,25,20,2]{1,3,2,0:T(2,128)}, u32[]{:S(2)}, u32[]{:S(2)}) collective-permute-start(f32[5,25,20,2]{1,3,2,0:T(2,128)S(1)} %copy.255), channel_id=1, source_target_pairs={{0,1},{1,2},{2,3},{4,5},{5,6},{6,7},{8,9},{9,10},{10,11},{12,13},{... | collective-permute-start | bytes 60008 | tf_op jit(solution)/shard_map/ppermute | solution.py:16
  106.0 5.7 %collective-permute-start.7 = (f32[5,25,20,2]{1,3,2,0:T(2,128)}, f32[5,25,20,2]{1,3,2,0:T(2,128)}, u32[]{:S(2)}, u32[]{:S(2)}) collective-permute-start(f32[5,25,20,2]{1,3,2,0:T(2,128)} %copy.256), channel_id=1, source_target_pairs={{1,0},{2,1},{3,2},{5,4},{6,5},{7,6},{9,8},{10,9},{11,10},{13,12},{... | collective-permute-start | bytes 60008 | tf_op jit(solution)/shard_map/ppermute | solution.py:17
  108.4 6.1 %copy-start.8 = (f32[5,25,2,256]{3,2,1,0:T(2,128)S(1)}, f32[5,25,2,256]{3,2,1,0:T(2,128)}, u32[]{:S(2)}) copy-start(f32[5,25,2,256]{3,2,1,0:T(2,128)} %copy-done.7) | copy-start | bytes 768004
  119.5 1.9 %copy-start = (f32[25,20,260]{2,1,0:T(8,128)}, f32[25,20,260]{2,1,0:T(8,128)S(1)}, u32[]{:S(2)}) copy-start(f32[25,20,260]{2,1,0:T(8,128)S(1)} %get-tuple-element.283) | copy-start | bytes 1560004
  127.4 10.1 %copy-start.14 = (f32[24,16,256]{2,1,0:T(8,128)}, f32[24,16,256]{2,1,0:T(8,128)S(1)}, u32[]{:S(2)}) copy-start(f32[24,16,256]{2,1,0:T(8,128)S(1)} %get-tuple-element.327) | copy-start | bytes 1179652
  127.4 10.1 %copy-start.9 = (f32[24,16,256]{2,1,0:T(8,128)}, f32[24,16,256]{2,1,0:T(8,128)S(1)}, u32[]{:S(2)}) copy-start(f32[24,16,256]{2,1,0:T(8,128)S(1)} %get-tuple-element.324) | copy-start | bytes 1179652
  128.5 9.0 %copy-start.11 = (f32[24,16,256]{2,1,0:T(8,128)}, f32[24,16,256]{2,1,0:T(8,128)S(1)}, u32[]{:S(2)}) copy-start(f32[24,16,256]{2,1,0:T(8,128)S(1)} %get-tuple-element.394) | copy-start | bytes 1179652
  128.5 8.9 %collective-permute-start.8 = (f32[2,25,2,256]{3,2,1,0:T(2,128)S(1)}, f32[2,25,2,256]{3,2,1,0:T(2,128)S(1)}, u32[]{:S(2)}, u32[]{:S(2)}) collective-permute-start(f32[2,25,2,256]{3,2,1,0:T(2,128)S(1)} %get-tuple-element.300), channel_id=1, source_target_pairs={{0,4},{4,8},{8,12},{12,16},{16,20},{20,24},{24,28},{1,5},{5,9},{9,... | collective-permute-start | bytes 307208 | tf_op jit(solution)/shard_map/ppermute | solution.py:16
  135.5 6.9 %collective-permute-start.9 = (f32[2,25,2,256]{3,2,1,0:T(2,128)S(1)}, f32[2,25,2,256]{3,2,1,0:T(2,128)S(1)}, u32[]{:S(2)}, u32[]{:S(2)}) collective-permute-start(f32[2,25,2,256]{3,2,1,0:T(2,128)S(1)} %get-tuple-element.301), channel_id=1, source_target_pairs={{4,0},{8,4},{12,8},{16,12},{20,16},{24,20},{28,24},{5,1},{9,5},{13... | collective-permute-start | bytes 307208 | tf_op jit(solution)/shard_map/ppermute | solution.py:17
  138.2 5.6 %copy-start.20 = (f32[2,25,2,256]{3,2,1,0:T(2,128)}, f32[2,25,2,256]{3,2,1,0:T(2,128)S(1)}, u32[]{:S(2)}) copy-start(f32[2,25,2,256]{3,2,1,0:T(2,128)S(1)} %collective-permute-done.8) | copy-start | bytes 307204
  142.6 8.9 %copy-start.10 = (f32[24,16,256]{2,1,0:T(8,128)S(1)}, f32[24,16,256]{2,1,0:T(8,128)}, u32[]{:S(2)}) copy-start(f32[24,16,256]{2,1,0:T(8,128)} %copy-done.9) | copy-start | bytes 1179652
  145.3 9.1 %collective-permute-start.10 = (f32[2,25,20,2]{1,3,2,0:T(2,128)S(1)}, f32[2,25,20,2]{1,3,2,0:T(2,128)S(1)}, u32[]{:S(2)}, u32[]{:S(2)}) collective-permute-start(f32[2,25,20,2]{1,3,2,0:T(2,128)S(1)} %copy.259), channel_id=1, source_target_pairs={{0,1},{1,2},{2,3},{4,5},{5,6},{6,7},{8,9},{9,10},{10,11},{12,13},{... | collective-permute-start | bytes 24008 | tf_op jit(solution)/shard_map/ppermute | solution.py:16
  150.0 5.6 %collective-permute-start.11 = (f32[2,25,20,2]{1,3,2,0:T(2,128)}, f32[2,25,20,2]{1,3,2,0:T(2,128)}, u32[]{:S(2)}, u32[]{:S(2)}) collective-permute-start(f32[2,25,20,2]{1,3,2,0:T(2,128)} %copy.260), channel_id=1, source_target_pairs={{1,0},{2,1},{3,2},{5,4},{6,5},{7,6},{9,8},{10,9},{11,10},{13,12},{... | collective-permute-start | bytes 24008 | tf_op jit(solution)/shard_map/ppermute | solution.py:17
  (13 other events, 14.5 us)
where the time goes:
time: 167 us; the launch traced here: 165 us
  blocking collectives  40.4 us (24%)
  local copies, waits for them, and re-layouts  32.3 us (19%)
  starting transfers between devices  31.4 us (19%)
  other arithmetic  27.4 us (16%)
  between operations  22.3 us (13%)
  waiting for transfers between devices  11.2 us (7%)
    psum x1, blocking collectives, conjugate(): m = list(lax.psum(jnp.stack(sums), ('trow', 'tcol')))  40.4 us
    ppermute x6, starting transfers between devices, padded_2(): before = lax.ppermute(last, axis, up)  20.9 us
    ppermute x6, waiting for transfers between devices, padded_2(): after = lax.ppermute(leading, axis, down)  11.2 us
    ppermute x6, starting transfers between devices, padded_2(): after = lax.ppermute(leading, axis, down)  10.5 us
    concatenate x6, other arithmetic, padded_2(): array = jnp.concatenate([before, array, after], axis=dim)  8.95 us
    slice x6, local copies, waits for them, and re-layouts, padded_2(): last = lax.slice_in_dim(array, length - width, length, axis=dim)  7.93 us
    another operation x2, local copies, waits for them, and re-layouts, conjugate(): m = list(lax.psum(jnp.stack(sums), ('trow', 'tcol')))  5.73 us
    ppermute x2, local copies, waits for them, and re-layouts, padded_2(): after = lax.ppermute(leading, axis, down)  4.85 us
  transfers between devices with their start and end apart: 12, of which 4 were waited for; matrix products, arithmetic and copies ran while one was open for 13% of the time, Pallas kernels for 0%

commit v1 on v0

v1 whole, which is shorter than its diff:
```python
import jax
import jax.numpy as jnp
from jax import lax
from jax.experimental import pallas as pl
from jax.experimental.pallas import tpu as pltpu
from jax.sharding import PartitionSpec as P

ITERS = 4


def padded_2(array, sides, width):
    for axis, dim in sides:
        peers, length = (lax.axis_size(axis), array.shape[dim])
        up = [(i, (i + 1) % peers) for i in range(peers - 1)]
        down = [(j, i) for i, j in up]
        last = lax.slice_in_dim(array, length - width, length, axis=dim)
        leading = lax.slice_in_dim(array, 0, width, axis=dim)
        before = lax.ppermute(last, axis, up)
        after = lax.ppermute(leading, axis, down)
        array = jnp.concatenate([before, array, after], axis=dim)
    return array


def cut_along(array, start, count, axis_index):
    return lax.slice_in_dim(array, start, start + count, axis=axis_index)


def join(before, array, after, axis):
    return jnp.concatenate([before, array, after], axis=axis)


def open_faces(velocity, wet, first, count, axis):
    return (
        cut_along(velocity, first, count, axis)
        * cut_along(wet, first, count, axis)
        * cut_along(wet, first + 1, count, axis)
    )


def forward_change(tracer, opened, axis, length):
    centre = cut_along(tracer, 1, length + 1, axis) + cut_along(tracer, 2, length + 1, axis)
    outer = cut_along(tracer, 0, length + 1, axis) + cut_along(tracer, 3, length + 1, axis)
    fluxes = opened * (7.0 * centre - outer) * (1.0 / 12.0)
    return cut_along(fluxes, 1, length, axis) - cut_along(fluxes, 0, length, axis)


def adjoint_change(field, opened, axis, length):
    faces = opened * (cut_along(field, 0, length + 3, axis) - cut_along(field, 1, length + 3, axis))
    return (
        7.0 * (cut_along(faces, 2, length, axis) + cut_along(faces, 1, length, axis))
        - cut_along(faces, 3, length, axis)
        - cut_along(faces, 0, length, axis)
    ) * (1.0 / 12.0)


def wet_at(land, bottom, k):
    return jnp.where(k < bottom[...], land[k].astype(jnp.float32), 0.0)


def couple_at(kappa, land, bottom, k, depth):
    below = jnp.minimum(k + 1, depth - 1)
    value = kappa[jnp.minimum(k, depth - 2)] * wet_at(land, bottom, k) * wet_at(land, bottom, below)
    return jnp.where(k < depth - 1, value, 0.0)


def rows_of(rb, ra, index, k, own):
    return join(rb[index, k], own, ra[index, k], 0)


def cols_of(rim, index, k, own):
    edge = rim[index, k]
    return join(edge[:, :2], own, edge[:, 2:], 1)


def forward_kernel(
    theta, salt, vx, vy, land, kappa, forcing, bottom, rb, ra, rim, theta_mix, salt_mix, ratios
):
    depth, rows, cols = theta.shape

    def down(k, carry):
        couple_before, ratio_before, theta_before, salt_before = carry
        wet = wet_at(land, bottom, k)
        couple = couple_at(kappa, land, bottom, k, depth)
        inverse = 1.0 / (1.0 + couple_before - couple_before * ratio_before + couple)
        ratio = couple * inverse
        ratios[k] = ratio
        open_x = open_faces(
            rows_of(rb, ra, 2, k, vx[k]), rows_of(rb, ra, 3, k, wet), 1, rows + 1, 0
        )
        open_y = open_faces(cols_of(rim, 2, k, vy[k]), cols_of(rim, 3, k, wet), 1, cols + 1, 1)
        found = []
        for index, (tracer, before) in enumerate(((theta, theta_before), (salt, salt_before))):
            own = tracer[k]
            masked = own * wet
            adv = (
                own
                - forward_change(rows_of(rb, ra, index, k, masked), open_x, 0, rows)
                - forward_change(cols_of(rim, index, k, masked), open_y, 1, cols)
            )
            if index == 0:
                adv = adv + jnp.where(k == 0, forcing[...] * wet, 0.0)
            found.append((adv + couple_before * before) * inverse)
        theta_mix[k] = found[0]
        salt_mix[k] = found[1]
        return couple, ratio, found[0], found[1]

    zero = jnp.zeros((rows, cols), jnp.float32)
    _, _, theta_last, salt_last = lax.fori_loop(0, depth, down, (zero, zero, zero, zero))

    def up(i, carry):
        k = depth - 2 - i
        a = theta_mix[k] + ratios[k] * carry[0]
        b = salt_mix[k] + ratios[k] * carry[1]
        theta_mix[k] = a
        salt_mix[k] = b
        return a, b

    lax.fori_loop(0, depth - 1, up, (theta_last, salt_last))


def mixing_kernel(
    theta_cot, salt_cot, land, kappa, bottom, zeta, theta_mix, salt_mix,
    theta_mu, salt_mu, kappa_grad, forcing_grad, ratios
):
    depth, rows, cols = theta_cot.shape

    def down(k, carry):
        couple_before, ratio_before, theta_before, salt_before = carry
        lifted = wet_at(land, bottom, k) * zeta[...]
        couple = couple_at(kappa, land, bottom, k, depth)
        inverse = 1.0 / (1.0 + couple_before - couple_before * ratio_before + couple)
        ratio = couple * inverse
        ratios[k] = ratio
        a = (theta_cot[k] + 0.2 * lifted + couple_before * theta_before) * inverse
        b = (salt_cot[k] - 0.15 * lifted + couple_before * salt_before) * inverse
        theta_mu[k] = a
        salt_mu[k] = b
        return couple, ratio, a, b

    zero = jnp.zeros((rows, cols), jnp.float32)
    _, _, theta_last, salt_last = lax.fori_loop(0, depth, down, (zero, zero, zero, zero))

    def up(i, carry):
        k = depth - 2 - i
        a = theta_mu[k] + ratios[k] * carry[0]
        b = salt_mu[k] + ratios[k] * carry[1]
        theta_mu[k] = a
        salt_mu[k] = b
        opened = wet_at(land, bottom, k) * wet_at(land, bottom, k + 1)
        kappa_grad[k] = -opened * (
            (a - carry[0]) * (theta_mix[k] - theta_mix[k + 1])
            + (b - carry[1]) * (salt_mix[k] - salt_mix[k + 1])
        )
        return a, b

    theta_top, _ = lax.fori_loop(0, depth - 1, up, (theta_last, salt_last))
    forcing_grad[...] = zeta[...] + wet_at(land, bottom, 0) * theta_top


def adjoint_kernel(
    theta_mu, salt_mu, vx, vy, land, bottom, rb, ra, rim, mu_rb, mu_ra, mu_rim, theta_grad, salt_grad
):
    depth, rows, cols = theta_mu.shape

    def level(k, carry):
        wet = wet_at(land, bottom, k)
        open_x = open_faces(
            rows_of(rb, ra, 2, k, vx[k]), rows_of(rb, ra, 3, k, wet), 0, rows + 3, 0
        )
        open_y = open_faces(cols_of(rim, 2, k, vy[k]), cols_of(rim, 3, k, wet), 0, cols + 3, 1)
        for index, (field, out) in enumerate(((theta_mu, theta_grad), (salt_mu, salt_grad))):
            own = field[k]
            out[k] = own - wet * (
                adjoint_change(rows_of(mu_rb, mu_ra, index, k, own), open_x, 0, rows)
                + adjoint_change(cols_of(mu_rim, index, k, own), open_y, 1, cols)
            )
        return carry

    lax.fori_loop(0, depth, level, 0)


LOW, HIGH = 0.2, 9.2
CENTRE, RADIUS = (HIGH + LOW) / 2, (HIGH - LOW) / 2


def times_operator(poly):
    out = [0.0] * (len(poly) + 1)
    for k, c in enumerate(poly):
        out[k] = out[k] + CENTRE * c
        if k == 0:
            out[1] = out[1] + RADIUS * c
        else:
            out[k + 1] = out[k + 1] + 0.5 * RADIUS * c
            out[k - 1] = out[k - 1] + 0.5 * RADIUS * c
    return out


def inner(p, q, moments):
    total = 0.0
    for i, a in enumerate(p):
        for j, b in enumerate(q):
            total = total + a * b * (0.5 * (moments[i + j] + moments[abs(i - j)]))
    return total


def add_scaled(p, scale, q):
    size = max(len(p), len(q))
    p = p + [0.0] * (size - len(p))
    q = q + [0.0] * (size - len(q))
    return [a + scale * b for a, b in zip(p, q)]


def weights_from(moments):
    residual = [jnp.ones_like(moments[0])]
    direction = residual
    result = []
    norm_now = moments[0]
    for iteration in range(ITERS):
        image = times_operator(direction)
        step = norm_now / inner(direction, image, moments)
        result = add_scaled(result, step, direction)
        if iteration + 1 < ITERS:
            residual = add_scaled(residual, -step, image)
            norm_next = inner(residual, residual, moments)
            direction = add_scaled(residual, norm_next / norm_now, direction)
            norm_now = norm_next
    return result


def conjugate(target, bottom, depth):
    rows, cols = target.shape
    rim = ITERS
    padded = padded_2(jnp.stack([target, bottom.astype(jnp.float32)]), (("trow", 1), ("tcol", 2)), rim)
    row = lax.broadcasted_iota(jnp.int32, (rows + 2 * rim, 1), 0) - rim + lax.axis_index("trow") * rows
    col = lax.broadcasted_iota(jnp.int32, (1, cols + 2 * rim), 1) - rim + lax.axis_index("tcol") * cols
    inside = ((row >= 0) & (row < rows * lax.axis_size("trow"))) & (
        (col >= 0) & (col < cols * lax.axis_size("tcol"))
    )
    scaled = (4.2 - CENTRE + padded[1] / depth) / RADIUS
    basis = [padded[0]]
    for k in range(ITERS):
        field = basis[-1]
        edge = k + 1
        beside = field[2:, 1:-1] + field[:-2, 1:-1] + field[1:-1, 2:] + field[1:-1, :-2]
        image = scaled[edge:-edge, edge:-edge] * field[1:-1, 1:-1] - beside * (1.0 / RADIUS)
        if k > 0:
            image = 2.0 * image - basis[-2][2:-2, 2:-2]
        basis.append(jnp.where(inside[edge:-edge, edge:-edge], image, 0.0))
    own = [f[rim - k : rim - k + rows, rim - k : rim - k + cols] for k, f in enumerate(basis)]
    sums = [jnp.sum(own[0] * own[k]) for k in range(5)]
    sums += [jnp.sum(own[2] * own[3]), jnp.sum(own[3] * own[3]), jnp.sum(own[3] * own[4])]
    m = list(lax.psum(jnp.stack(sums), ("trow", "tcol")))
    m = m[:5] + [2.0 * m[5] - m[1], 2.0 * m[6] - m[0], 2.0 * m[7] - m[1]]
    weights = weights_from(m)
    result = weights[0] * own[0]
    for k in range(1, ITERS):
        result = result + weights[k] * own[k]
    return result


def call(kernel, outs, scratch, args):
    size = sum(a.size for a in args) * 4
    return pl.pallas_call(
        kernel,
        out_shape=[jax.ShapeDtypeStruct(o, jnp.float32) for o in outs],
        in_specs=[pl.BlockSpec(memory_space=pltpu.VMEM)] * len(args),
        out_specs=[pl.BlockSpec(memory_space=pltpu.VMEM)] * len(outs),
        scratch_shapes=[pltpu.VMEM(o, jnp.float32) for o in scratch],
        compiler_params=pltpu.CompilerParams(vmem_limit_bytes=40 * 1024 * 1024),
        cost_estimate=pl.CostEstimate(flops=size * 20, bytes_accessed=size, transcendentals=0),
    )(*args)


def from_neighbours(first, last, axis):
    peers = lax.axis_size(axis)
    up = [(i, (i + 1) % peers) for i in range(peers - 1)]
    down = [(j, i) for i, j in up]
    return lax.ppermute(last, axis, up), lax.ppermute(first, axis, down)


def row_rims(fields):
    return from_neighbours(
        jnp.stack([f[:, :2] for f in fields]), jnp.stack([f[:, -2:] for f in fields]), "trow"
    )


def col_rims(fields):
    before, after = from_neighbours(
        jnp.stack([f[:, :, :2].swapaxes(1, 2) for f in fields]),
        jnp.stack([f[:, :, -2:].swapaxes(1, 2) for f in fields]),
        "tcol",
    )
    return jnp.concatenate([before, after], axis=2).swapaxes(2, 3)


def shards(
    theta,
    salt,
    velocity_x,
    velocity_y,
    land_mask,
    kappa,
    forcing,
    bottom,
    theta_cot,
    salt_cot,
    surface_cot,
):
    depth, rows, cols = theta.shape
    levels = lax.broadcasted_iota(jnp.int32, (depth, 1, 1), 0)
    wet = land_mask.astype(jnp.float32) * (levels < bottom[None]).astype(jnp.float32)
    rb, ra = row_rims([theta * wet, salt * wet, velocity_x, wet])
    rim = col_rims([theta * wet, salt * wet, velocity_y, wet])
    whole = (depth, rows, cols)
    theta_mix, salt_mix = call(
        forward_kernel,
        [whole, whole],
        [whole],
        (theta, salt, velocity_x, velocity_y, land_mask, kappa, forcing, bottom, rb, ra, rim),
    )
    zeta = conjugate(surface_cot, bottom, depth)
    theta_mu, salt_mu, kappa_grad, forcing_grad = call(
        mixing_kernel,
        [whole, whole, (depth - 1, rows, cols), (rows, cols)],
        [whole],
        (theta_cot, salt_cot, land_mask, kappa, bottom, zeta, theta_mix, salt_mix),
    )
    mu_rb, mu_ra = row_rims([theta_mu, salt_mu])
    mu_rim = col_rims([theta_mu, salt_mu])
    theta_grad, salt_grad = call(
        adjoint_kernel,
        [whole, whole],
        [],
        (theta_mu, salt_mu, velocity_x, velocity_y, land_mask, bottom, rb, ra, rim, mu_rb, mu_ra, mu_rim),
    )
    return (theta_grad, salt_grad, kappa_grad, forcing_grad)


def solution(mesh):
    in_specs = (
        P(None, "trow", "tcol"),
        P(None, "trow", "tcol"),
        P(None, "trow", "tcol"),
        P(None, "trow", "tcol"),
        P(None, "trow", "tcol"),
        P(None, "trow", "tcol"),
        P("trow", "tcol"),
        P("trow", "tcol"),
        P(None, "trow", "tcol"),
        P(None, "trow", "tcol"),
        P("trow", "tcol"),
    )
    out_specs = (
        P(None, "trow", "tcol"),
        P(None, "trow", "tcol"),
        P(None, "trow", "tcol"),
        P("trow", "tcol"),
    )
    return jax.shard_map(shards, mesh=mesh, in_specs=in_specs, out_specs=out_specs, check_vma=False)
```

time: 167 us -> 158 us (0.946)
  Pallas kernels: 0 us -> 22.9 us
  other arithmetic: 27.4 us -> 11.5 us
  local copies, waits for them, and re-layouts: 32.3 us -> 21 us
  waiting for transfers between devices: 11.2 us -> 6.44 us
  starting transfers between devices: 31.4 us -> 33.8 us
  between operations: 22.3 us -> 20.3 us
    ppermute x0 -> x8, starting transfers between devices: none -> 24.2 us  [from_neighbours(): return (lax.ppermute(last, axis, up), lax.ppermute(first, axis, down))]
    pallas_call x0 -> x3, Pallas kernels: none -> 22.9 us  [call(): pl.pallas_call(kernel, out_shape=[jax.ShapeDtypeStruct(o, jnp.float32) fo...]
    ppermute x6 -> x2, starting transfers between devices: 20.9 us -> 6.24 us  [padded_2(): before = lax.ppermute(last, axis, up)]
    ppermute x4 -> x0, local copies, waits for them, and re-layouts: 8.93 us -> none  [the longest x2 4.85 us: padded_2(): after = lax.ppermute(leading, axis, down)]
    another operation x5 -> x18, local copies, waits for them, and re-layouts: 0.05 us -> 8.59 us  [the longest x9 4.34 us: col_rims(): jnp.stack([f[:, :, -2:].swapaxes(1, 2) for f in fields])]
    ppermute x6 -> x2, waiting for transfers between devices: 11.2 us -> 2.97 us  [padded_2(): after = lax.ppermute(leading, axis, down)]
    slice x6 -> x1, local copies, waits for them, and re-layouts: 7.93 us -> 0.07 us  [padded_2(): last = lax.slice_in_dim(array, length - width, length, axis=dim)]
    concatenate x6 -> x2, other arithmetic: 8.95 us -> 1.51 us  [padded_2(): array = jnp.concatenate([before, array, after], axis=dim)]
  transfers between devices with their start and end apart: 12 -> 12, of which waited for: 4 -> 2; matrix products, arithmetic and copies ran while one was open for 13% -> 17% of each run, Pallas kernels for 0% -> 0%
where the time goes in v1:
time: 158 us; the launch traced here: 156 us
  blocking collectives  40.3 us (26%)
  starting transfers between devices  33.8 us (21%)
  Pallas kernels  22.9 us (14%)
  local copies, waits for them, and re-layouts  21 us (13%)
  between operations  20.3 us (13%)
  other arithmetic  11.5 us (7%)
  waiting for transfers between devices  6.44 us (4%)
    psum x1, blocking collectives, conjugate(): m = list(lax.psum(jnp.stack(sums), ('trow', 'tcol')))  40.3 us
    ppermute x8, starting transfers between devices, from_neighbours(): return (lax.ppermute(last, axis, up), lax.ppermute(first, axis, down))  24.2 us
    pallas_call x3, Pallas kernels, call(): pl.pallas_call(kernel, out_shape=[jax.ShapeDtypeStruct(o, jnp.float32) fo...  22.9 us
    ppermute x2, starting transfers between devices, padded_2(): before = lax.ppermute(last, axis, up)  6.24 us
    another operation x2, local copies, waits for them, and re-layouts, conjugate(): m = list(lax.psum(jnp.stack(sums), ('trow', 'tcol')))  5.83 us
    another operation x9, local copies, waits for them, and re-layouts, col_rims(): jnp.stack([f[:, :, -2:].swapaxes(1, 2) for f in fields])  4.34 us
    ppermute x8, waiting for transfers between devices, from_neighbours(): return (lax.ppermute(last, axis, up), lax.ppermute(first, axis, down))  3.47 us
    another operation x5, local copies, waits for them, and re-layouts, col_rims(): jnp.stack([f[:, :, :2].swapaxes(1, 2) for f in fields])  3.42 us
  transfers between devices with their start and end apart: 12, of which 2 were waited for; matrix products, arithmetic and copies ran while one was open for 17% of the time, Pallas kernels for 0%

profile of v1, /device:TPU:3, one launch (start us, length us, event | category | flops | bytes accessed | tf_op | source)
XLA Modules:
  0.0 156.3 jit_solution(6452908514252364049)
XLA Ops:
  2.0 3.7 %collective-permute-start = (f32[2,4,256]{2,1,0:T(4,128)}, f32[2,4,256]{2,1,0:T(4,128)S(1)}, u32[]{:S(2)}, u32[]{:S(2)}) collective-permute-start(f32[2,4,256]{2,1,0:T(4,128)} %get-tuple-element.58), channel_id=1, source_target_pairs={{0,4},{4,8},{8,12},{12,16},{16,20},{20,24},{24,28},{1,5},{5,9},{9,... | collective-permute-start | bytes 24584 | tf_op jit(solution)/shard_map/ppermute | solution.py:18
  5.7 2.1 %collective-permute-start.1 = (f32[2,4,256]{2,1,0:T(4,128)}, f32[2,4,256]{2,1,0:T(4,128)}, u32[]{:S(2)}, u32[]{:S(2)}) collective-permute-start(f32[2,4,256]{2,1,0:T(4,128)} %get-tuple-element.59), channel_id=1, source_target_pairs={{4,0},{8,4},{12,8},{16,12},{20,16},{24,20},{28,24},{5,1},{9,5},{13... | collective-permute-start | bytes 24584 | tf_op jit(solution)/shard_map/ppermute | solution.py:19
  7.7 1.1 fusion.23
  13.4 1.4 pad_maximum_fusion.7
  14.8 1.3 collective-permute-start.7
  18.4 4.6 %collective-permute-start.6 = (f32[4,25,2,16]{1,3,2,0:T(8,128)}, f32[4,25,2,16]{1,3,2,0:T(8,128)}, u32[]{:S(2)}, u32[]{:S(2)}) collective-permute-start(f32[4,25,2,16]{1,3,2,0:T(8,128)} %pad_maximum_fusion.6), channel_id=1, source_target_pairs={{0,1},{1,2},{2,3},{4,5},{5,6},{6,7},{8,9},{9,10},{10,11},{12,13},{... | collective-permute-start | bytes 38408 | tf_op jit(solution)/shard_map/ppermute | solution.py:278
  24.0 5.1 %collective-permute-start.4 = (f32[4,25,2,256]{3,2,1,0:T(2,128)}, f32[4,25,2,256]{3,2,1,0:T(2,128)S(1)}, u32[]{:S(2)}, u32[]{:S(2)}) collective-permute-start(f32[4,25,2,256]{3,2,1,0:T(2,128)} %pad_maximum_fusion), channel_id=1, source_target_pairs={{0,4},{4,8},{8,12},{12,16},{16,20},{20,24},{24,28},{1,5},{5,9},{9,... | collective-permute-start | bytes 614408 | tf_op jit(solution)/shard_map/ppermute | solution.py:278
  30.0 2.6 %collective-permute-start.2 = (f32[2,24,4]{2,1,0:T(8,128)S(1)}, f32[2,24,4]{2,1,0:T(8,128)S(1)}, u32[]{:S(2)}, u32[]{:S(2)}) collective-permute-start(f32[2,24,4]{2,1,0:T(8,128)S(1)} %get-tuple-element.56), channel_id=1, source_target_pairs={{0,1},{1,2},{2,3},{4,5},{5,6},{6,7},{8,9},{9,10},{10,11},{12,13},{... | collective-permute-start | bytes 2312 | tf_op jit(solution)/shard_map/ppermute | solution.py:18
  32.6 1.3 collective-permute-start.3
  34.7 3.0 %collective-permute-done.3 = f32[2,24,4]{2,1,0:T(8,128)S(1)} collective-permute-done((f32[2,24,4]{2,1,0:T(8,128)S(1)}, f32[2,24,4]{2,1,0:T(8,128)S(1)}, u32[]{:S(2)}, u32[]{:S(2)}) %collective-permute-start.3) | collective-permute-done | bytes 800 | tf_op jit(solution)/shard_map/ppermute | solution.py:19
  39.7 5.2 %stack.143 = f32[8]{0:T(128)S(1)} concatenate(f32[1]{0:T(128)} %bitcast.3, f32[1]{0:T(128)} %bitcast.5, f32[1]{0:T(128)} %bitcast.6, f32[1]{0:T(128)} %bitcast.7, f32[1]{0:T(128)} %bitcast.8, f32[1]{0:T(128)} %bitcast.9, f32[1]{0:T(128)} %bitcast.10, f32[1]{0:T(128)} %bitcast.11), dimensions={0} | concatenate | bytes 64 | tf_op jit(solution)/shard_map/stack | solution.py:252
  44.9 1.9 %collective-permute-start.5 = (f32[4,25,2,256]{3,2,1,0:T(2,128)}, f32[4,25,2,256]{3,2,1,0:T(2,128)}, u32[]{:S(2)}, u32[]{:S(2)}) collective-permute-start(f32[4,25,2,256]{3,2,1,0:T(2,128)} %pad_maximum_fusion.1), channel_id=1, source_target_pairs={{4,0},{8,4},{12,8},{16,12},{20,16},{24,20},{28,24},{5,1},{9,5},{13... | collective-permute-start | bytes 614408 | tf_op jit(solution)/shard_map/ppermute | solution.py:278
  46.8 40.3 %psum.7 = f32[8]{0:T(128)S(1)} all-reduce(f32[8]{0:T(128)S(1)} %stack.143), channel_id=1, replica_groups=mesh['trow'=8,'tcol'=4] {'trow','tcol'}, use_global_device_ids=true, to_apply=%region_8.9 | all-reduce | flops 8 | bytes 64 | tf_op jit(solution)/shard_map/psum | solution.py:252
  107.2 1.5 pad_maximum_fusion.2
  108.7 1.5 copy.23
  110.3 10.7 %shard_map.138 = (f32[25,16,256]{2,1,0:T(8,128)S(1)}, f32[25,16,256]{2,1,0:T(8,128)S(1)}) custom-call(f32[25,16,256]{2,1,0:T(8,128)S(1)} %copy-done.3, f32[25,16,256]{2,1,0:T(8,128)S(1)} %copy-done.4, f32[25,16,256]{2,1,0:T(8,128)S(1)} %copy-done.2, f32[25,16,256]{2,1,0:T(8,128)S(1)} %copy-done.1, s32[25,16,256]{2,1,0:T(8,128)S(1)} %copy-done, ...), custom_call_target="tpu_custom_call" | custom-call | flops 58183680 | bytes 2909184 | tf_op jit(solution)/shard_map/pallas_call | solution.py:263
  121.0 1.6 %shard_map.139 = (f32[25,16,256]{2,1,0:T(8,128)S(1)}, f32[25,16,256]{2,1,0:T(8,128)S(1)}, f32[24,16,256]{2,1,0:T(8,128)}, f32[16,256]{1,0:T(8,128)}) custom-call(f32[25,16,256]{2,1,0:T(8,128)S(1)} %copy-done.7, f32[25,16,256]{2,1,0:T(8,128)S(1)} %copy-done.8, s32[25,16,256]{2,1,0:T(8,128)S(1)} %copy-done, f32[24,16,256]{2,1,0:T(8,128)S(1)} %copy-done.5, ...), custom_call_target="tpu_custom_call" | custom-call | flops 49479680 | bytes 2473984 | tf_op jit(solution)/shard_map/pallas_call | solution.py:263
  124.9 4.0 %collective-permute-start.8 = (f32[2,25,2,256]{3,2,1,0:T(2,128)}, f32[2,25,2,256]{3,2,1,0:T(2,128)}, u32[]{:S(2)}, u32[]{:S(2)}) collective-permute-start(f32[2,25,2,256]{3,2,1,0:T(2,128)} %pad_maximum_fusion.3), channel_id=1, source_target_pairs={{0,4},{4,8},{8,12},{12,16},{16,20},{20,24},{24,28},{1,5},{5,9},{9,... | collective-permute-start | bytes 307208 | tf_op jit(solution)/shard_map/ppermute | solution.py:278
  132.4 1.4 collective-permute-start.11
  133.8 4.0 %collective-permute-start.10 = (f32[2,25,2,16]{1,3,2,0:T(8,128)S(1)}, f32[2,25,2,16]{1,3,2,0:T(8,128)S(1)}, u32[]{:S(2)}, u32[]{:S(2)}) collective-permute-start(f32[2,25,2,16]{1,3,2,0:T(8,128)S(1)} %pad_maximum_fusion.10), channel_id=1, source_target_pairs={{0,1},{1,2},{2,3},{4,5},{5,6},{6,7},{8,9},{9,10},{10,11},{12,13},{... | collective-permute-start | bytes 19208 | tf_op jit(solution)/shard_map/ppermute | solution.py:278
  138.5 1.9 %collective-permute-start.9 = (f32[2,25,2,256]{3,2,1,0:T(2,128)}, f32[2,25,2,256]{3,2,1,0:T(2,128)}, u32[]{:S(2)}, u32[]{:S(2)}) collective-permute-start(f32[2,25,2,256]{3,2,1,0:T(2,128)} %pad_maximum_fusion.4), channel_id=1, source_target_pairs={{4,0},{8,4},{12,8},{16,12},{20,16},{24,20},{28,24},{5,1},{9,5},{13... | collective-permute-start | bytes 307208 | tf_op jit(solution)/shard_map/ppermute | solution.py:278
  141.1 1.2 copy.28
  142.3 3.4 %collective-permute-done.9.mu_ra = f32[2,25,2,256]{3,2,1,0:T(2,128)} collective-permute-done((f32[2,25,2,256]{3,2,1,0:T(2,128)}, f32[2,25,2,256]{3,2,1,0:T(2,128)}, u32[]{:S(2)}, u32[]{:S(2)}) %collective-permute-start.9) | collective-permute-done | bytes 102432 | tf_op jit(solution)/shard_map/ppermute | solution.py:278
  145.7 10.6 %shard_map.140 = (f32[25,16,256]{2,1,0:T(8,128)}, f32[25,16,256]{2,1,0:T(8,128)}) custom-call(f32[25,16,256]{2,1,0:T(8,128)S(1)} %get-tuple-element.14.theta_mu, f32[25,16,256]{2,1,0:T(8,128)S(1)} %get-tuple-element.15.salt_mu, f32[25,16,256]{2,1,0:T(8,128)S(1)} %copy-done.2, f32[25,16,256]{2,1,0:T(8,128)S(1)} %copy-done.1, s32[25,16,256]{2,1,0:T(8,128)S(1)} %copy-done, ...), custom_call_target="tpu_custom_call" | custom-call | flops 54343680 | bytes 2717184 | tf_op jit(solution)/shard_map/pallas_call | solution.py:263
  (87 shorter events, 20.7 us)
Async XLA Ops:
  2.0 27.2 %collective-permute-start = (f32[2,4,256]{2,1,0:T(4,128)}, f32[2,4,256]{2,1,0:T(4,128)S(1)}, u32[]{:S(2)}, u32[]{:S(2)}) collective-permute-start(f32[2,4,256]{2,1,0:T(4,128)} %get-tuple-element.58), channel_id=1, source_target_pairs={{0,4},{4,8},{8,12},{12,16},{16,20},{20,24},{24,28},{1,5},{5,9},{9,... | collective-permute-start | bytes 24584 | tf_op jit(solution)/shard_map/ppermute | solution.py:18
  5.7 3.5 %copy-start = (s32[25,16,256]{2,1,0:T(8,128)S(1)}, s32[25,16,256]{2,1,0:T(8,128)}, u32[]{:S(2)}) copy-start(s32[25,16,256]{2,1,0:T(8,128)} %land.5) | copy-start | bytes 1228804
  5.7 3.4 %copy-start.3 = (f32[25,16,256]{2,1,0:T(8,128)S(1)}, f32[25,16,256]{2,1,0:T(8,128)}, u32[]{:S(2)}) copy-start(f32[25,16,256]{2,1,0:T(8,128)} %theta.1) | copy-start | bytes 1228804
  5.7 23.5 %collective-permute-start.1 = (f32[2,4,256]{2,1,0:T(4,128)}, f32[2,4,256]{2,1,0:T(4,128)}, u32[]{:S(2)}, u32[]{:S(2)}) collective-permute-start(f32[2,4,256]{2,1,0:T(4,128)} %get-tuple-element.59), channel_id=1, source_target_pairs={{4,0},{8,4},{12,8},{16,12},{20,16},{24,20},{28,24},{5,1},{9,5},{13... | collective-permute-start | bytes 24584 | tf_op jit(solution)/shard_map/ppermute | solution.py:19
  9.6 1.0 copy-start.4
  14.8 92.4 %collective-permute-start.7 = (f32[4,25,2,16]{1,3,2,0:T(8,128)}, f32[4,25,2,16]{1,3,2,0:T(8,128)}, u32[]{:S(2)}, u32[]{:S(2)}) collective-permute-start(f32[4,25,2,16]{1,3,2,0:T(8,128)} %pad_maximum_fusion.7), channel_id=1, source_target_pairs={{1,0},{2,1},{3,2},{5,4},{6,5},{7,6},{9,8},{10,9},{11,10},{13,12},{... | collective-permute-start | bytes 38408 | tf_op jit(solution)/shard_map/ppermute | solution.py:278
  17.3 5.8 %copy-start.2 = (f32[25,16,256]{2,1,0:T(8,128)S(1)}, f32[25,16,256]{2,1,0:T(8,128)}, u32[]{:S(2)}) copy-start(f32[25,16,256]{2,1,0:T(8,128)} %vx.3) | copy-start | bytes 1228804
  18.4 88.7 %collective-permute-start.6 = (f32[4,25,2,16]{1,3,2,0:T(8,128)}, f32[4,25,2,16]{1,3,2,0:T(8,128)}, u32[]{:S(2)}, u32[]{:S(2)}) collective-permute-start(f32[4,25,2,16]{1,3,2,0:T(8,128)} %pad_maximum_fusion.6), channel_id=1, source_target_pairs={{0,1},{1,2},{2,3},{4,5},{5,6},{6,7},{8,9},{9,10},{10,11},{12,13},{... | collective-permute-start | bytes 38408 | tf_op jit(solution)/shard_map/ppermute | solution.py:278
  24.0 86.2 %collective-permute-start.4 = (f32[4,25,2,256]{3,2,1,0:T(2,128)}, f32[4,25,2,256]{3,2,1,0:T(2,128)S(1)}, u32[]{:S(2)}, u32[]{:S(2)}) collective-permute-start(f32[4,25,2,256]{3,2,1,0:T(2,128)} %pad_maximum_fusion), channel_id=1, source_target_pairs={{0,4},{4,8},{8,12},{12,16},{16,20},{20,24},{24,28},{1,5},{5,9},{9,... | collective-permute-start | bytes 614408 | tf_op jit(solution)/shard_map/ppermute | solution.py:278
  30.0 4.7 %collective-permute-start.2 = (f32[2,24,4]{2,1,0:T(8,128)S(1)}, f32[2,24,4]{2,1,0:T(8,128)S(1)}, u32[]{:S(2)}, u32[]{:S(2)}) collective-permute-start(f32[2,24,4]{2,1,0:T(8,128)S(1)} %get-tuple-element.56), channel_id=1, source_target_pairs={{0,1},{1,2},{2,3},{4,5},{5,6},{6,7},{8,9},{9,10},{10,11},{12,13},{... | collective-permute-start | bytes 2312 | tf_op jit(solution)/shard_map/ppermute | solution.py:18
  32.6 5.0 %collective-permute-start.3 = (f32[2,24,4]{2,1,0:T(8,128)S(1)}, f32[2,24,4]{2,1,0:T(8,128)S(1)}, u32[]{:S(2)}, u32[]{:S(2)}) collective-permute-start(f32[2,24,4]{2,1,0:T(8,128)S(1)} %get-tuple-element.57), channel_id=1, source_target_pairs={{1,0},{2,1},{3,2},{5,4},{6,5},{7,6},{9,8},{10,9},{11,10},{13,12},{... | collective-permute-start | bytes 2312 | tf_op jit(solution)/shard_map/ppermute | solution.py:19
  44.9 65.4 %collective-permute-start.5 = (f32[4,25,2,256]{3,2,1,0:T(2,128)}, f32[4,25,2,256]{3,2,1,0:T(2,128)}, u32[]{:S(2)}, u32[]{:S(2)}) collective-permute-start(f32[4,25,2,256]{3,2,1,0:T(2,128)} %pad_maximum_fusion.1), channel_id=1, source_target_pairs={{4,0},{8,4},{12,8},{16,12},{20,16},{24,20},{28,24},{5,1},{9,5},{13... | collective-permute-start | bytes 614408 | tf_op jit(solution)/shard_map/ppermute | solution.py:278
  108.7 1.5 copy-start.1
  108.7 1.5 copy-start.5
  108.7 1.5 copy-start.9
  110.3 10.7 %copy-start.7 = (f32[25,16,256]{2,1,0:T(8,128)S(1)}, f32[25,16,256]{2,1,0:T(8,128)}, u32[]{:S(2)}) copy-start(f32[25,16,256]{2,1,0:T(8,128)} %theta_cot.1) | copy-start | bytes 1228804
  110.3 10.7 %copy-start.8 = (f32[25,16,256]{2,1,0:T(8,128)S(1)}, f32[25,16,256]{2,1,0:T(8,128)}, u32[]{:S(2)}) copy-start(f32[25,16,256]{2,1,0:T(8,128)} %salt_cot.1) | copy-start | bytes 1228804
  124.9 17.3 %collective-permute-start.8 = (f32[2,25,2,256]{3,2,1,0:T(2,128)}, f32[2,25,2,256]{3,2,1,0:T(2,128)}, u32[]{:S(2)}, u32[]{:S(2)}) collective-permute-start(f32[2,25,2,256]{3,2,1,0:T(2,128)} %pad_maximum_fusion.3), channel_id=1, source_target_pairs={{0,4},{4,8},{8,12},{12,16},{16,20},{20,24},{24,28},{1,5},{5,9},{9,... | collective-permute-start | bytes 307208 | tf_op jit(solution)/shard_map/ppermute | solution.py:278
  129.7 1.9 %copy-start.10 = (f32[1,25,2,16]{2,3,1,0:T(8,128)S(1)}, f32[1,25,2,16]{2,3,1,0:T(8,128)}, u32[]{:S(2)}) copy-start(f32[1,25,2,16]{2,3,1,0:T(8,128)} %get-tuple-element.33) | copy-start | bytes 9604
  131.6 2.2 %copy-start.13 = (f32[1,25,2,16]{1,3,2,0:T(8,128)S(1)}, f32[1,25,2,16]{1,3,2,0:T(8,128)}, u32[]{:S(2)}) copy-start(f32[1,25,2,16]{1,3,2,0:T(8,128)} %copy.24) | copy-start | bytes 9604
  132.4 5.5 %copy-start.11 = (f32[1,25,2,256]{3,2,1,0:T(2,128)S(1)}, f32[1,25,2,256]{3,2,1,0:T(2,128)}, u32[]{:S(2)}) copy-start(f32[1,25,2,256]{3,2,1,0:T(2,128)} %get-tuple-element.36) | copy-start | bytes 153604
  132.4 8.1 %collective-permute-start.11 = (f32[2,25,2,16]{1,3,2,0:T(8,128)S(1)}, f32[2,25,2,16]{1,3,2,0:T(8,128)S(1)}, u32[]{:S(2)}, u32[]{:S(2)}) collective-permute-start(f32[2,25,2,16]{1,3,2,0:T(8,128)S(1)} %pad_maximum_fusion.11), channel_id=1, source_target_pairs={{1,0},{2,1},{3,2},{5,4},{6,5},{7,6},{9,8},{10,9},{11,10},{13,12},{... | collective-permute-start | bytes 19208 | tf_op jit(solution)/shard_map/ppermute | solution.py:278
  133.8 6.6 %collective-permute-start.10 = (f32[2,25,2,16]{1,3,2,0:T(8,128)S(1)}, f32[2,25,2,16]{1,3,2,0:T(8,128)S(1)}, u32[]{:S(2)}, u32[]{:S(2)}) collective-permute-start(f32[2,25,2,16]{1,3,2,0:T(8,128)S(1)} %pad_maximum_fusion.10), channel_id=1, source_target_pairs={{0,1},{1,2},{2,3},{4,5},{5,6},{6,7},{8,9},{9,10},{10,11},{12,13},{... | collective-permute-start | bytes 19208 | tf_op jit(solution)/shard_map/ppermute | solution.py:278
  138.5 7.2 %collective-permute-start.9 = (f32[2,25,2,256]{3,2,1,0:T(2,128)}, f32[2,25,2,256]{3,2,1,0:T(2,128)}, u32[]{:S(2)}, u32[]{:S(2)}) collective-permute-start(f32[2,25,2,256]{3,2,1,0:T(2,128)} %pad_maximum_fusion.4), channel_id=1, source_target_pairs={{4,0},{8,4},{12,8},{16,12},{20,16},{24,20},{28,24},{5,1},{9,5},{13... | collective-permute-start | bytes 307208 | tf_op jit(solution)/shard_map/ppermute | solution.py:278
  (4 other events, 2.9 us)

commit v2 on v1

--- a/solution.py
+++ b/solution.py
@@ -1,3 +1,4 @@
+import functools
 import jax
 import jax.numpy as jnp
 from jax import lax
@@ -227,6 +228,73 @@
     return result
 
 
+MESH = pl.DeviceIdType.MESH
+
+
+def gather_kernel(lanes, piece, out, line, plane, own_sem, send, recv):
+    rows, cols = lax.axis_size("trow"), lax.axis_size("tcol")
+    row, col = lax.axis_index("trow"), lax.axis_index("tcol")
+    peers = [(row, lax.rem(col + d, cols)) for d in range(1, cols)]
+    peers += [(lax.rem(row + d, rows), col) for d in range(1, rows)]
+    barrier = pltpu.get_barrier_semaphore()
+    for peer in peers:
+        pl.semaphore_signal(barrier, inc=1, device_id=peer, device_id_type=MESH)
+    keep = pltpu.make_async_copy(piece, line.at[0], own_sem.at[0])
+    keep.start()
+    keep.wait()
+    pl.semaphore_wait(barrier, len(peers))
+
+    def remote(src, dst, index):
+        return pltpu.make_async_remote_copy(
+            src_ref=src,
+            dst_ref=dst,
+            send_sem=send.at[index],
+            recv_sem=recv.at[index],
+            device_id=peers[index],
+            device_id_type=MESH,
+        )
+
+    along = [remote(piece, line.at[d], d - 1) for d in range(1, cols)]
+    for copy in along:
+        copy.start()
+    for copy in along:
+        copy.wait()
+    across = [remote(line, plane.at[d - 1], cols + d - 2) for d in range(1, rows)]
+    for copy in across:
+        copy.start()
+    total = line[0]
+    for d in range(1, cols):
+        total = total + line[d]
+    for copy in across:
+        copy.wait()
+    for d in range(rows - 1):
+        for e in range(cols):
+            total = total + plane[d, e]
+    out[...] = total
+
+
+def sum_everywhere(sums):
+    rows, cols = lax.axis_size("trow"), lax.axis_size("tcol")
+    lanes = 128
+    piece = jnp.broadcast_to(jnp.pad(sums, (0, lanes - sums.shape[0]))[None], (8, lanes))
+    count = rows + cols - 2
+    total = pl.pallas_call(
+        functools.partial(gather_kernel, lanes),
+        out_shape=jax.ShapeDtypeStruct((8, lanes), jnp.float32),
+        in_specs=[pl.BlockSpec(memory_space=pltpu.VMEM)],
+        out_specs=pl.BlockSpec(memory_space=pltpu.VMEM),
+        scratch_shapes=[
+            pltpu.VMEM((cols, 8, lanes), jnp.float32),
+            pltpu.VMEM((rows - 1, cols, 8, lanes), jnp.float32),
+            pltpu.SemaphoreType.DMA((1,)),
+            pltpu.SemaphoreType.DMA((count,)),
+            pltpu.SemaphoreType.DMA((count,)),
+        ],
+        compiler_params=pltpu.CompilerParams(collective_id=0, has_side_effects=True),
+    )(piece)
+    return total[0, : sums.shape[0]]
+
+
 def conjugate(target, bottom, depth):
     rows, cols = target.shape
     rim = ITERS
@@ -249,7 +317,7 @@
     own = [f[rim - k : rim - k + rows, rim - k : rim - k + cols] for k, f in enumerate(basis)]
     sums = [jnp.sum(own[0] * own[k]) for k in range(5)]
     sums += [jnp.sum(own[2] * own[3]), jnp.sum(own[3] * own[3]), jnp.sum(own[3] * own[4])]
-    m = list(lax.psum(jnp.stack(sums), ("trow", "tcol")))
+    m = list(sum_everywhere(jnp.stack(sums)))
     m = m[:5] + [2.0 * m[5] - m[1], 2.0 * m[6] - m[0], 2.0 * m[7] - m[1]]
     weights = weights_from(m)
     result = weights[0] * own[0]

time: 158 us -> 129 us (0.82)
  blocking collectives: 40.3 us -> 0 us
  Pallas kernels: 22.9 us -> 35.1 us
  waiting for transfers between devices: 6.44 us -> 4.5 us
    psum x1 -> x0, blocking collectives: 40.3 us -> none  [conjugate(): m = list(lax.psum(jnp.stack(sums), ('trow', 'tcol')))]
    pallas_call x0 -> x1, Pallas kernels: none -> 12.2 us  [sum_everywhere(): pl.pallas_call(functools.partial(gather_kernel, lanes), out_shape=jax.Sha...]
    ppermute x2, waiting for transfers between devices: 2.97 us -> 1.03 us  [padded_2(): after = lax.ppermute(leading, axis, down)]
  transfers between devices with their start and end apart: 12 -> 12, of which waited for: 2 -> 2; matrix products, arithmetic and copies ran while one was open for 17% -> 22% of each run, Pallas kernels for 0% -> 10%
where the time goes in v2:
time: 129 us; the launch traced here: 127 us
  Pallas kernels  35.1 us (27%)
  starting transfers between devices  32.8 us (25%)
  local copies, waits for them, and re-layouts  22.4 us (17%)
  between operations  20.8 us (16%)
  other arithmetic  11.5 us (9%)
  waiting for transfers between devices  4.5 us (3%)
    ppermute x8, starting transfers between devices, from_neighbours(): return (lax.ppermute(last, axis, up), lax.ppermute(first, axis, down))  23.2 us
    pallas_call x3, Pallas kernels, call(): pl.pallas_call(kernel, out_shape=[jax.ShapeDtypeStruct(o, jnp.float32) fo...  22.9 us
    pallas_call x1, Pallas kernels, sum_everywhere(): pl.pallas_call(functools.partial(gather_kernel, lanes), out_shape=jax.Sha...  12.2 us
    another operation x2, local copies, waits for them, and re-layouts, conjugate(): m = list(sum_everywhere(jnp.stack(sums)))  6.6 us
    ppermute x2, starting transfers between devices, padded_2(): before = lax.ppermute(last, axis, up)  6.26 us
    another operation x9, local copies, waits for them, and re-layouts, col_rims(): jnp.stack([f[:, :, -2:].swapaxes(1, 2) for f in fields])  4.34 us
    ppermute x8, waiting for transfers between devices, from_neighbours(): return (lax.ppermute(last, axis, up), lax.ppermute(first, axis, down))  3.47 us
    another operation x5, local copies, waits for them, and re-layouts, col_rims(): jnp.stack([f[:, :, :2].swapaxes(1, 2) for f in fields])  3.42 us
  transfers between devices with their start and end apart: 12, of which 2 were waited for; matrix products, arithmetic and copies ran while one was open for 22% of the time, Pallas kernels for 10%

profile of v2, /device:TPU:3, one launch (start us, length us, event | category | flops | bytes accessed | tf_op | source)
XLA Modules:
  0.0 127.0 jit_solution(1504643972608212589)
XLA Ops:
  2.0 3.7 %collective-permute-start = (f32[2,4,256]{2,1,0:T(4,128)}, f32[2,4,256]{2,1,0:T(4,128)S(1)}, u32[]{:S(2)}, u32[]{:S(2)}) collective-permute-start(f32[2,4,256]{2,1,0:T(4,128)} %get-tuple-element.58), channel_id=1, source_target_pairs={{0,4},{4,8},{8,12},{12,16},{16,20},{20,24},{24,28},{1,5},{5,9},{9,... | collective-permute-start | bytes 24584 | tf_op jit(solution)/shard_map/ppermute | solution.py:19
  5.7 2.1 %collective-permute-start.1 = (f32[2,4,256]{2,1,0:T(4,128)}, f32[2,4,256]{2,1,0:T(4,128)}, u32[]{:S(2)}, u32[]{:S(2)}) collective-permute-start(f32[2,4,256]{2,1,0:T(4,128)} %get-tuple-element.59), channel_id=1, source_target_pairs={{4,0},{8,4},{12,8},{16,12},{20,16},{24,20},{28,24},{5,1},{9,5},{13... | collective-permute-start | bytes 24584 | tf_op jit(solution)/shard_map/ppermute | solution.py:20
  7.7 1.1 fusion.23
  13.4 1.4 %pad_maximum_fusion.7 = f32[4,25,2,16]{1,3,2,0:T(8,128)} fusion(f32[1,25,2,16]{1,3,2,0:T(8,128)} %copy.22, f32[1,25,2,16]{1,3,2,0:T(8,128)S(1)} %bitcast.101, f32[1,25,2,16]{1,3,2,0:T(8,128)} %copy.21, f32[1,25,2,16]{1,3,2,0:T(8,128)} %copy.20), kind=kLoop, calls=%fused_computation.19 | loop fusion | flops 9600 | bytes 25600 | tf_op jit(solution)/shard_map/stack | solution.py:357
  14.8 1.3 %collective-permute-start.7 = (f32[4,25,2,16]{1,3,2,0:T(8,128)}, f32[4,25,2,16]{1,3,2,0:T(8,128)}, u32[]{:S(2)}, u32[]{:S(2)}) collective-permute-start(f32[4,25,2,16]{1,3,2,0:T(8,128)} %pad_maximum_fusion.7), channel_id=1, source_target_pairs={{1,0},{2,1},{3,2},{5,4},{6,5},{7,6},{9,8},{10,9},{11,10},{13,12},{... | collective-permute-start | bytes 38408 | tf_op jit(solution)/shard_map/ppermute | solution.py:346
  18.4 4.6 %collective-permute-start.6 = (f32[4,25,2,16]{1,3,2,0:T(8,128)}, f32[4,25,2,16]{1,3,2,0:T(8,128)}, u32[]{:S(2)}, u32[]{:S(2)}) collective-permute-start(f32[4,25,2,16]{1,3,2,0:T(8,128)} %pad_maximum_fusion.6), channel_id=1, source_target_pairs={{0,1},{1,2},{2,3},{4,5},{5,6},{6,7},{8,9},{9,10},{10,11},{12,13},{... | collective-permute-start | bytes 38408 | tf_op jit(solution)/shard_map/ppermute | solution.py:346
  24.0 5.1 %collective-permute-start.4 = (f32[4,25,2,256]{3,2,1,0:T(2,128)}, f32[4,25,2,256]{3,2,1,0:T(2,128)S(1)}, u32[]{:S(2)}, u32[]{:S(2)}) collective-permute-start(f32[4,25,2,256]{3,2,1,0:T(2,128)} %pad_maximum_fusion), channel_id=1, source_target_pairs={{0,4},{4,8},{8,12},{12,16},{16,20},{20,24},{24,28},{1,5},{5,9},{9,... | collective-permute-start | bytes 614408 | tf_op jit(solution)/shard_map/ppermute | solution.py:346
  30.0 2.6 %collective-permute-start.2 = (f32[2,24,4]{2,1,0:T(8,128)S(1)}, f32[2,24,4]{2,1,0:T(8,128)S(1)}, u32[]{:S(2)}, u32[]{:S(2)}) collective-permute-start(f32[2,24,4]{2,1,0:T(8,128)S(1)} %get-tuple-element.56), channel_id=1, source_target_pairs={{0,1},{1,2},{2,3},{4,5},{5,6},{6,7},{8,9},{9,10},{10,11},{12,13},{... | collective-permute-start | bytes 2312 | tf_op jit(solution)/shard_map/ppermute | solution.py:19
  32.6 1.3 %collective-permute-start.3 = (f32[2,24,4]{2,1,0:T(8,128)S(1)}, f32[2,24,4]{2,1,0:T(8,128)S(1)}, u32[]{:S(2)}, u32[]{:S(2)}) collective-permute-start(f32[2,24,4]{2,1,0:T(8,128)S(1)} %get-tuple-element.57), channel_id=1, source_target_pairs={{1,0},{2,1},{3,2},{5,4},{6,5},{7,6},{9,8},{10,9},{11,10},{13,12},{... | collective-permute-start | bytes 2312 | tf_op jit(solution)/shard_map/ppermute | solution.py:20
  34.6 1.9 %collective-permute-start.5 = (f32[4,25,2,256]{3,2,1,0:T(2,128)}, f32[4,25,2,256]{3,2,1,0:T(2,128)}, u32[]{:S(2)}, u32[]{:S(2)}) collective-permute-start(f32[4,25,2,256]{3,2,1,0:T(2,128)} %pad_maximum_fusion.1), channel_id=1, source_target_pairs={{4,0},{8,4},{12,8},{16,12},{20,16},{24,20},{28,24},{5,1},{9,5},{13... | collective-permute-start | bytes 614408 | tf_op jit(solution)/shard_map/ppermute | solution.py:346
  39.6 5.0 %stack.143 = f32[8]{0:T(128)S(1)} concatenate(f32[1]{0:T(128)} %bitcast.3, f32[1]{0:T(128)} %bitcast.5, f32[1]{0:T(128)} %bitcast.6, f32[1]{0:T(128)} %bitcast.7, f32[1]{0:T(128)} %bitcast.8, f32[1]{0:T(128)} %bitcast.9, f32[1]{0:T(128)} %bitcast.10, f32[1]{0:T(128)} %bitcast.11), dimensions={0} | concatenate | bytes 64 | tf_op jit(solution)/shard_map/stack | solution.py:320
  45.2 12.2 %shard_map.138 = f32[8,128]{1,0:T(8,128)} custom-call(f32[8,128]{1,0:T(8,128)} %broadcast_in_dim.27.piece), custom_call_target="tpu_custom_call" | custom-call | tf_op jit(solution)/shard_map/pallas_call | solution.py:281
  57.4 1.6 %fusion.25 = (f32[1,1]{1,0:T(1,128)}, f32[1,1]{1,0:T(1,128)}, f32[1,1]{1,0:T(1,128)}, f32[1,1]{1,0:T(1,128)}, f32[1,1]{1,0:T(1,128)}, /*index=5*/f32[1,1]{1,0:T(1,128)}, f32[1,1]{1,0:T(1,128)}, f32[1,1]{1,0:T(1,128)}) fusion(f32[8,128]{1,0:T(8,128)} %shard_map.138), kind=kLoop, calls=%fused_computation.96 | loop fusion | bytes 64 | tf_op jit(solution)/shard_map/unstack | solution.py:320
  78.9 1.5 %pad_maximum_fusion.2 = f32[4,25,4,16]{1,3,2,0:T(8,128)} fusion(f32[4,25,2,16]{1,3,2,0:T(8,128)} %collective-permute-done.7, f32[4,25,2,16]{1,3,2,0:T(8,128)} %collective-permute-done.6), kind=kLoop, calls=%fused_computation.14 | loop fusion | flops 6400 | bytes 51200 | tf_op jit(solution)/shard_map/concatenate | solution.py:361
  80.4 1.5 %copy.23 = f32[4,25,4,16]{2,3,1,0:T(8,128)S(1)} copy(f32[4,25,4,16]{1,3,2,0:T(8,128)} %pad_maximum_fusion.2) | data formatting | bytes 51200 | tf_op jit(solution)/shard_map/concatenate | solution.py:361
  82.0 10.7 %shard_map.139 = (f32[25,16,256]{2,1,0:T(8,128)S(1)}, f32[25,16,256]{2,1,0:T(8,128)S(1)}) custom-call(f32[25,16,256]{2,1,0:T(8,128)S(1)} %copy-done.3, f32[25,16,256]{2,1,0:T(8,128)S(1)} %copy-done.4, f32[25,16,256]{2,1,0:T(8,128)S(1)} %copy-done.2, f32[25,16,256]{2,1,0:T(8,128)S(1)} %copy-done.1, s32[25,16,256]{2,1,0:T(8,128)S(1)} %copy-done, ...), custom_call_target="tpu_custom_call" | custom-call | flops 58183680 | bytes 2909184 | tf_op jit(solution)/shard_map/pallas_call | solution.py:331
  92.7 1.6 %shard_map.140 = (f32[25,16,256]{2,1,0:T(8,128)S(1)}, f32[25,16,256]{2,1,0:T(8,128)S(1)}, f32[24,16,256]{2,1,0:T(8,128)}, f32[16,256]{1,0:T(8,128)}) custom-call(f32[25,16,256]{2,1,0:T(8,128)S(1)} %copy-done.7, f32[25,16,256]{2,1,0:T(8,128)S(1)} %copy-done.8, s32[25,16,256]{2,1,0:T(8,128)S(1)} %copy-done, f32[24,16,256]{2,1,0:T(8,128)S(1)} %copy-done.5, ...), custom_call_target="tpu_custom_call" | custom-call | flops 49479680 | bytes 2473984 | tf_op jit(solution)/shard_map/pallas_call | solution.py:331
  96.7 3.0 %collective-permute-start.8 = (f32[2,25,2,256]{3,2,1,0:T(2,128)}, f32[2,25,2,256]{3,2,1,0:T(2,128)}, u32[]{:S(2)}, u32[]{:S(2)}) collective-permute-start(f32[2,25,2,256]{3,2,1,0:T(2,128)} %pad_maximum_fusion.3), channel_id=1, source_target_pairs={{0,4},{4,8},{8,12},{12,16},{16,20},{20,24},{24,28},{1,5},{5,9},{9,... | collective-permute-start | bytes 307208 | tf_op jit(solution)/shard_map/ppermute | solution.py:346
  103.1 1.4 %collective-permute-start.11 = (f32[2,25,2,16]{1,3,2,0:T(8,128)S(1)}, f32[2,25,2,16]{1,3,2,0:T(8,128)S(1)}, u32[]{:S(2)}, u32[]{:S(2)}) collective-permute-start(f32[2,25,2,16]{1,3,2,0:T(8,128)S(1)} %pad_maximum_fusion.11), channel_id=1, source_target_pairs={{1,0},{2,1},{3,2},{5,4},{6,5},{7,6},{9,8},{10,9},{11,10},{13,12},{... | collective-permute-start | bytes 19208 | tf_op jit(solution)/shard_map/ppermute | solution.py:346
  104.6 4.0 %collective-permute-start.10 = (f32[2,25,2,16]{1,3,2,0:T(8,128)S(1)}, f32[2,25,2,16]{1,3,2,0:T(8,128)S(1)}, u32[]{:S(2)}, u32[]{:S(2)}) collective-permute-start(f32[2,25,2,16]{1,3,2,0:T(8,128)S(1)} %pad_maximum_fusion.10), channel_id=1, source_target_pairs={{0,1},{1,2},{2,3},{4,5},{5,6},{6,7},{8,9},{9,10},{10,11},{12,13},{... | collective-permute-start | bytes 19208 | tf_op jit(solution)/shard_map/ppermute | solution.py:346
  109.3 1.9 %collective-permute-start.9 = (f32[2,25,2,256]{3,2,1,0:T(2,128)}, f32[2,25,2,256]{3,2,1,0:T(2,128)}, u32[]{:S(2)}, u32[]{:S(2)}) collective-permute-start(f32[2,25,2,256]{3,2,1,0:T(2,128)} %pad_maximum_fusion.4), channel_id=1, source_target_pairs={{4,0},{8,4},{12,8},{16,12},{20,16},{24,20},{28,24},{5,1},{9,5},{13... | collective-permute-start | bytes 307208 | tf_op jit(solution)/shard_map/ppermute | solution.py:346
  111.9 1.2 copy.28
  113.0 3.4 %collective-permute-done.9.mu_ra = f32[2,25,2,256]{3,2,1,0:T(2,128)} collective-permute-done((f32[2,25,2,256]{3,2,1,0:T(2,128)}, f32[2,25,2,256]{3,2,1,0:T(2,128)}, u32[]{:S(2)}, u32[]{:S(2)}) %collective-permute-start.9) | collective-permute-done | bytes 102432 | tf_op jit(solution)/shard_map/ppermute | solution.py:346
  116.5 10.6 %shard_map.141 = (f32[25,16,256]{2,1,0:T(8,128)}, f32[25,16,256]{2,1,0:T(8,128)}) custom-call(f32[25,16,256]{2,1,0:T(8,128)S(1)} %get-tuple-element.14.theta_mu, f32[25,16,256]{2,1,0:T(8,128)S(1)} %get-tuple-element.15.salt_mu, f32[25,16,256]{2,1,0:T(8,128)S(1)} %copy-done.2, f32[25,16,256]{2,1,0:T(8,128)S(1)} %copy-done.1, s32[25,16,256]{2,1,0:T(8,128)S(1)} %copy-done, ...), custom_call_target="tpu_custom_call" | custom-call | flops 54343680 | bytes 2717184 | tf_op jit(solution)/shard_map/pallas_call | solution.py:331
  (89 shorter events, 21.6 us)
Async XLA Ops:
  2.0 27.2 %collective-permute-start = (f32[2,4,256]{2,1,0:T(4,128)}, f32[2,4,256]{2,1,0:T(4,128)S(1)}, u32[]{:S(2)}, u32[]{:S(2)}) collective-permute-start(f32[2,4,256]{2,1,0:T(4,128)} %get-tuple-element.58), channel_id=1, source_target_pairs={{0,4},{4,8},{8,12},{12,16},{16,20},{20,24},{24,28},{1,5},{5,9},{9,... | collective-permute-start | bytes 24584 | tf_op jit(solution)/shard_map/ppermute | solution.py:19
  5.7 3.5 %copy-start = (s32[25,16,256]{2,1,0:T(8,128)S(1)}, s32[25,16,256]{2,1,0:T(8,128)}, u32[]{:S(2)}) copy-start(s32[25,16,256]{2,1,0:T(8,128)} %land.5) | copy-start | bytes 1228804
  5.7 3.4 %copy-start.3 = (f32[25,16,256]{2,1,0:T(8,128)S(1)}, f32[25,16,256]{2,1,0:T(8,128)}, u32[]{:S(2)}) copy-start(f32[25,16,256]{2,1,0:T(8,128)} %theta.1) | copy-start | bytes 1228804
  5.7 23.5 %collective-permute-start.1 = (f32[2,4,256]{2,1,0:T(4,128)}, f32[2,4,256]{2,1,0:T(4,128)}, u32[]{:S(2)}, u32[]{:S(2)}) collective-permute-start(f32[2,4,256]{2,1,0:T(4,128)} %get-tuple-element.59), channel_id=1, source_target_pairs={{4,0},{8,4},{12,8},{16,12},{20,16},{24,20},{28,24},{5,1},{9,5},{13... | collective-permute-start | bytes 24584 | tf_op jit(solution)/shard_map/ppermute | solution.py:20
  9.6 1.0 copy-start.4
  14.8 64.1 %collective-permute-start.7 = (f32[4,25,2,16]{1,3,2,0:T(8,128)}, f32[4,25,2,16]{1,3,2,0:T(8,128)}, u32[]{:S(2)}, u32[]{:S(2)}) collective-permute-start(f32[4,25,2,16]{1,3,2,0:T(8,128)} %pad_maximum_fusion.7), channel_id=1, source_target_pairs={{1,0},{2,1},{3,2},{5,4},{6,5},{7,6},{9,8},{10,9},{11,10},{13,12},{... | collective-permute-start | bytes 38408 | tf_op jit(solution)/shard_map/ppermute | solution.py:346
  17.3 5.8 %copy-start.2 = (f32[25,16,256]{2,1,0:T(8,128)S(1)}, f32[25,16,256]{2,1,0:T(8,128)}, u32[]{:S(2)}) copy-start(f32[25,16,256]{2,1,0:T(8,128)} %vx.3) | copy-start | bytes 1228804
  18.4 60.5 %collective-permute-start.6 = (f32[4,25,2,16]{1,3,2,0:T(8,128)}, f32[4,25,2,16]{1,3,2,0:T(8,128)}, u32[]{:S(2)}, u32[]{:S(2)}) collective-permute-start(f32[4,25,2,16]{1,3,2,0:T(8,128)} %pad_maximum_fusion.6), channel_id=1, source_target_pairs={{0,1},{1,2},{2,3},{4,5},{5,6},{6,7},{8,9},{9,10},{10,11},{12,13},{... | collective-permute-start | bytes 38408 | tf_op jit(solution)/shard_map/ppermute | solution.py:346
  24.0 58.0 %collective-permute-start.4 = (f32[4,25,2,256]{3,2,1,0:T(2,128)}, f32[4,25,2,256]{3,2,1,0:T(2,128)S(1)}, u32[]{:S(2)}, u32[]{:S(2)}) collective-permute-start(f32[4,25,2,256]{3,2,1,0:T(2,128)} %pad_maximum_fusion), channel_id=1, source_target_pairs={{0,4},{4,8},{8,12},{12,16},{16,20},{20,24},{24,28},{1,5},{5,9},{9,... | collective-permute-start | bytes 614408 | tf_op jit(solution)/shard_map/ppermute | solution.py:346
  30.0 4.7 %collective-permute-start.2 = (f32[2,24,4]{2,1,0:T(8,128)S(1)}, f32[2,24,4]{2,1,0:T(8,128)S(1)}, u32[]{:S(2)}, u32[]{:S(2)}) collective-permute-start(f32[2,24,4]{2,1,0:T(8,128)S(1)} %get-tuple-element.56), channel_id=1, source_target_pairs={{0,1},{1,2},{2,3},{4,5},{5,6},{6,7},{8,9},{9,10},{10,11},{12,13},{... | collective-permute-start | bytes 2312 | tf_op jit(solution)/shard_map/ppermute | solution.py:19
  32.6 5.0 %collective-permute-start.3 = (f32[2,24,4]{2,1,0:T(8,128)S(1)}, f32[2,24,4]{2,1,0:T(8,128)S(1)}, u32[]{:S(2)}, u32[]{:S(2)}) collective-permute-start(f32[2,24,4]{2,1,0:T(8,128)S(1)} %get-tuple-element.57), channel_id=1, source_target_pairs={{1,0},{2,1},{3,2},{5,4},{6,5},{7,6},{9,8},{10,9},{11,10},{13,12},{... | collective-permute-start | bytes 2312 | tf_op jit(solution)/shard_map/ppermute | solution.py:20
  34.6 47.3 %collective-permute-start.5 = (f32[4,25,2,256]{3,2,1,0:T(2,128)}, f32[4,25,2,256]{3,2,1,0:T(2,128)}, u32[]{:S(2)}, u32[]{:S(2)}) collective-permute-start(f32[4,25,2,256]{3,2,1,0:T(2,128)} %pad_maximum_fusion.1), channel_id=1, source_target_pairs={{4,0},{8,4},{12,8},{16,12},{20,16},{24,20},{28,24},{5,1},{9,5},{13... | collective-permute-start | bytes 614408 | tf_op jit(solution)/shard_map/ppermute | solution.py:346
  80.4 1.5 %copy-start.1 = (f32[25,16,256]{2,1,0:T(8,128)S(1)}, f32[25,16,256]{2,1,0:T(8,128)}, u32[]{:S(2)}) copy-start(f32[25,16,256]{2,1,0:T(8,128)} %vy.3) | copy-start | bytes 1228804
  80.4 1.5 %copy-start.5 = (f32[24,16,256]{2,1,0:T(8,128)S(1)}, f32[24,16,256]{2,1,0:T(8,128)}, u32[]{:S(2)}) copy-start(f32[24,16,256]{2,1,0:T(8,128)} %kappa.3) | copy-start | bytes 1179652
  80.4 1.5 %copy-start.9 = (f32[16,256]{1,0:T(8,128)S(1)}, f32[16,256]{1,0:T(8,128)}, u32[]{:S(2)}) copy-start(f32[16,256]{1,0:T(8,128)} %forcing.1) | copy-start | bytes 49156
  82.0 10.7 %copy-start.7 = (f32[25,16,256]{2,1,0:T(8,128)S(1)}, f32[25,16,256]{2,1,0:T(8,128)}, u32[]{:S(2)}) copy-start(f32[25,16,256]{2,1,0:T(8,128)} %theta_cot.1) | copy-start | bytes 1228804
  82.0 10.7 %copy-start.8 = (f32[25,16,256]{2,1,0:T(8,128)S(1)}, f32[25,16,256]{2,1,0:T(8,128)}, u32[]{:S(2)}) copy-start(f32[25,16,256]{2,1,0:T(8,128)} %salt_cot.1) | copy-start | bytes 1228804
  96.7 16.4 %collective-permute-start.8 = (f32[2,25,2,256]{3,2,1,0:T(2,128)}, f32[2,25,2,256]{3,2,1,0:T(2,128)}, u32[]{:S(2)}, u32[]{:S(2)}) collective-permute-start(f32[2,25,2,256]{3,2,1,0:T(2,128)} %pad_maximum_fusion.3), channel_id=1, source_target_pairs={{0,4},{4,8},{8,12},{12,16},{16,20},{20,24},{24,28},{1,5},{5,9},{9,... | collective-permute-start | bytes 307208 | tf_op jit(solution)/shard_map/ppermute | solution.py:346
  100.5 1.9 %copy-start.10 = (f32[1,25,2,16]{2,3,1,0:T(8,128)S(1)}, f32[1,25,2,16]{2,3,1,0:T(8,128)}, u32[]{:S(2)}) copy-start(f32[1,25,2,16]{2,3,1,0:T(8,128)} %get-tuple-element.33) | copy-start | bytes 9604
  102.4 2.2 %copy-start.13 = (f32[1,25,2,16]{1,3,2,0:T(8,128)S(1)}, f32[1,25,2,16]{1,3,2,0:T(8,128)}, u32[]{:S(2)}) copy-start(f32[1,25,2,16]{1,3,2,0:T(8,128)} %copy.24) | copy-start | bytes 9604
  103.1 5.5 %copy-start.11 = (f32[1,25,2,256]{3,2,1,0:T(2,128)S(1)}, f32[1,25,2,256]{3,2,1,0:T(2,128)}, u32[]{:S(2)}) copy-start(f32[1,25,2,256]{3,2,1,0:T(2,128)} %get-tuple-element.36) | copy-start | bytes 153604
  103.1 8.1 %collective-permute-start.11 = (f32[2,25,2,16]{1,3,2,0:T(8,128)S(1)}, f32[2,25,2,16]{1,3,2,0:T(8,128)S(1)}, u32[]{:S(2)}, u32[]{:S(2)}) collective-permute-start(f32[2,25,2,16]{1,3,2,0:T(8,128)S(1)} %pad_maximum_fusion.11), channel_id=1, source_target_pairs={{1,0},{2,1},{3,2},{5,4},{6,5},{7,6},{9,8},{10,9},{11,10},{13,12},{... | collective-permute-start | bytes 19208 | tf_op jit(solution)/shard_map/ppermute | solution.py:346
  104.6 6.6 %collective-permute-start.10 = (f32[2,25,2,16]{1,3,2,0:T(8,128)S(1)}, f32[2,25,2,16]{1,3,2,0:T(8,128)S(1)}, u32[]{:S(2)}, u32[]{:S(2)}) collective-permute-start(f32[2,25,2,16]{1,3,2,0:T(8,128)S(1)} %pad_maximum_fusion.10), channel_id=1, source_target_pairs={{0,1},{1,2},{2,3},{4,5},{5,6},{6,7},{8,9},{9,10},{10,11},{12,13},{... | collective-permute-start | bytes 19208 | tf_op jit(solution)/shard_map/ppermute | solution.py:346
  109.3 7.2 %collective-permute-start.9 = (f32[2,25,2,256]{3,2,1,0:T(2,128)}, f32[2,25,2,256]{3,2,1,0:T(2,128)}, u32[]{:S(2)}, u32[]{:S(2)}) collective-permute-start(f32[2,25,2,256]{3,2,1,0:T(2,128)} %pad_maximum_fusion.4), channel_id=1, source_target_pairs={{4,0},{8,4},{12,8},{16,12},{20,16},{24,20},{28,24},{5,1},{9,5},{13... | collective-permute-start | bytes 307208 | tf_op jit(solution)/shard_map/ppermute | solution.py:346
  (4 other events, 2.9 us)
